TPU v7x, 32 devices: a whole 2x2x4 slice. The times are simulated.
32 devices in a mesh: dp: 16 (over z, x, core), tensor: 2 (over y).
Axes of the slice: x: 2, y: 2, z: 4, core: 2. Of those that a mesh axis runs over, the one named last changes fastest.
Arguments:
- tokens: bfloat16 [2048, 1024], P(('dp', 'tensor')), may hold values from -6 to 6
- out_grad: bfloat16 [2048, 1024], P(('dp', 'tensor')), may hold values from -6 to 6
- lengths: int32 [16, 6], P('dp'), may hold values from 1 to 64, 128 in all within a row
- routes: int32 [2048, 8], P('dp'), may hold values from 0 to 31, all different within a row; in each aligned block of 128 rows (0 to 127, 128 to 255, ...) at most 48 rows name the same one
- attn_gain: float32 [1024], replicated, may hold values from 0.25 to 1.75
- w_query: bfloat16 [1024, 1024], P('dp', 'tensor'), may hold values from -0.1875 to 0.1875
- w_key: bfloat16 [1024, 512], P('dp', 'tensor'), may hold values from -0.1875 to 0.1875
- w_value: bfloat16 [1024, 512], P('dp', 'tensor'), may hold values from -0.1875 to 0.1875
- w_out: bfloat16 [1024, 1024], P('dp', 'tensor'), may hold values from -3 to 3
- ffn_gain: float32 [1024], replicated, may hold values from 0.25 to 1.75
- w_router: float32 [1024, 32], replicated, may hold values from -0.1875 to 0.1875
- w_gate: bfloat16 [32, 1024, 512], P(None, 'dp', 'tensor'), may hold values from -0.1875 to 0.1875
- w_up: bfloat16 [32, 1024, 512], P(None, 'dp', 'tensor'), may hold values from -0.1875 to 0.1875
- w_down: bfloat16 [32, 1024, 512], P(None, 'dp', 'tensor'), may hold values from -3 to 3
Outputs:
- block_out: bfloat16 [2048, 1024], P(('dp', 'tensor'))
- tokens_grad: float32 [2048, 1024], P(('dp', 'tensor'))
- attn_gain_grad: float32 [1024], replicated
- w_query_grad: float32 [1024, 1024], P('dp', 'tensor')
- w_key_grad: float32 [1024, 512], P('dp', 'tensor')
- w_value_grad: float32 [1024, 512], P('dp', 'tensor')
- w_out_grad: float32 [1024, 1024], P('dp', 'tensor')
- ffn_gain_grad: float32 [1024], replicated
- w_router_grad: float32 [1024, 32], replicated
- w_gate_grad: float32 [32, 1024, 512], P(None, 'dp', 'tensor')
- w_up_grad: float32 [32, 1024, 512], P(None, 'dp', 'tensor')
- w_down_grad: float32 [32, 1024, 512], P(None, 'dp', 'tensor')
Inputs may be any that keep to these rules, and one draw needn't show every extreme that they name: Each group's lengths sum to 128. `routes`: each row names 8 different experts; within the rows of one dp group no expert is named more than 48 times.
All inputs are finite; a program needn't handle non-finite values.
Results may differ from a plain program's by a relative error of at most 0.012.
The roundings to bfloat16 on the way count: a program that leaves them out, or rounds other values in their place, can miss the bound.
Values may be sent and summed in bfloat16 or wider, within the bound.
A program may use at most 128 MiB of HBM per device.

v0:
```python
import jax
import jax.numpy as jnp
from jax import lax
from jax.sharding import PartitionSpec as P

EXPERTS = 32
TOPK = 8
HEAD_DIM = 64
MOST = 48


eps_norm = 1e-06
residual_scale = 0.22
score_scale = 0.015625
rope_base = 10000.0
masked_score = -1e30


def norm_forward(row_block, gain_vec):
    rscale = lax.rsqrt(jnp.mean(row_block * row_block, axis=1, keepdims=True) + eps_norm)
    unit_rows = row_block * rscale
    return (unit_rows, rscale, (unit_rows * gain_vec).astype(jnp.bfloat16))


def norm_backward(gradient, unit_rows, rscale, gain_vec):
    unit_grad = gradient * gain_vec
    back_rows = rscale * (
        unit_grad - unit_rows * jnp.mean(unit_grad * unit_rows, axis=1, keepdims=True)
    )
    return (back_rows, jnp.sum(gradient * unit_rows, axis=0))


def seq_layout(seq_lengths, row_count):
    seq_ends = jnp.cumsum(seq_lengths)
    starts = seq_ends - seq_lengths
    places = jnp.arange(row_count, dtype=jnp.int32)
    segment = jnp.sum((places[:, None] >= seq_ends[None, :]).astype(jnp.int32), axis=1)
    member = segment[:, None] == jnp.arange(seq_lengths.shape[0], dtype=jnp.int32)[None, :]
    offset = jnp.sum(jnp.where(member, starts[None, :], 0), axis=1)
    allowed = (segment[:, None] == segment[None, :]) & (places[None, :] <= places[:, None])
    return (places - offset, allowed)


def rope_tables(position, head_width):
    frequency = rope_base ** (-(jnp.arange(head_width // 2, dtype=jnp.float32) * 2.0) / head_width)
    angles = position.astype(jnp.float32)[:, None] * frequency[None, :]
    cosine = jnp.concatenate([jnp.cos(angles), jnp.cos(angles)], axis=1)[:, None, :]
    sine_table = jnp.concatenate([jnp.sin(angles), jnp.sin(angles)], axis=1)[:, None, :]
    return (cosine, sine_table)


def rotate(vectors, cosine, sine_table):
    half_width = vectors.shape[-1] // 2
    first_half = vectors[..., :half_width]
    second_half = vectors[..., half_width:]
    return vectors * cosine + jnp.concatenate([-second_half, first_half], axis=-1) * sine_table


def unrotate(gradient, cosine, sine_table):
    half_width = gradient.shape[-1] // 2
    first_half = gradient[..., :half_width]
    second_half = gradient[..., half_width:]
    return gradient * cosine + jnp.concatenate([second_half, -first_half], axis=-1) * sine_table


def score_block(query_heads, key_heads, allowed):
    row_count, head_count, head_width = query_heads.shape
    kv_count = key_heads.shape[1]
    grouped = query_heads.reshape(row_count, kv_count, head_count // kv_count, head_width)
    scores = (
        jnp.einsum("igrd,jgd->grij", grouped, key_heads, preferred_element_type=jnp.float32)
        * score_scale
    )
    return (grouped, jnp.where(allowed[None, None], scores, masked_score))


def attend(query_heads, key_heads, value_heads, allowed):
    row_count, head_count, head_width = query_heads.shape
    grouped, scores = score_block(query_heads, key_heads, allowed)
    row_max = jnp.max(scores, axis=-1, keepdims=True)
    log_total = row_max + jnp.log(jnp.sum(jnp.exp(scores - row_max), axis=-1, keepdims=True))
    prob_bf = jnp.exp(scores - log_total).astype(jnp.bfloat16)
    mixed_out = jnp.einsum(
        "grij,jgd->igrd", prob_bf, value_heads, preferred_element_type=jnp.float32
    )
    return (mixed_out.reshape(row_count, head_count * head_width).astype(jnp.bfloat16), log_total)


def attend_back(query_heads, key_heads, value_heads, allowed, log_total, mixed_grad):
    row_count, head_count, head_width = query_heads.shape
    kv_count = key_heads.shape[1]
    grouped, scores = score_block(query_heads, key_heads, allowed)
    prob_full = jnp.exp(scores - log_total)
    grad_heads = mixed_grad.reshape(row_count, kv_count, head_count // kv_count, head_width)
    dprobs = jnp.einsum(
        "igrd,jgd->grij", grad_heads, value_heads, preferred_element_type=jnp.float32
    )
    row_delta = jnp.sum(prob_full * dprobs, axis=-1, keepdims=True)
    dscores = (prob_full * (dprobs - row_delta)).astype(jnp.bfloat16)
    dquery = (
        jnp.einsum("grij,jgd->igrd", dscores, key_heads, preferred_element_type=jnp.float32)
        * score_scale
    )
    key_grad = (
        jnp.einsum("grij,igrd->jgd", dscores, grouped, preferred_element_type=jnp.float32)
        * score_scale
    )
    dvalues = jnp.einsum(
        "grij,igrd->jgd",
        prob_full.astype(jnp.bfloat16),
        grad_heads,
        preferred_element_type=jnp.float32,
    )
    return (dquery.reshape(row_count, head_count, head_width), key_grad, dvalues)


def spread_rows(row_block):
    return lax.all_gather(row_block, "tensor", axis=0, tiled=True)


def narrow(partial_rows):
    return lax.psum_scatter(partial_rows, "tensor", scatter_dimension=0, tiled=True)


def local(
    tokens,
    out_grad,
    lengths,
    routes,
    attn_gain,
    w_query,
    w_key,
    w_value,
    w_out,
    ffn_gain,
    w_router,
    w_gate,
    w_up,
    w_down,
):
    local_rows = tokens.shape[0]
    row_count = routes.shape[0]
    model_width = tokens.shape[1]
    dp_count = lax.axis_size("dp")
    replicas = max(1, dp_count // EXPERTS)
    holders = max(1, EXPERTS // dp_count)
    clusters = EXPERTS // holders
    capacity = MOST // replicas
    half_ff = w_gate.shape[2]
    heads_here = w_query.shape[1] // HEAD_DIM
    kv_here = w_key.shape[1] // HEAD_DIM
    own_row = lax.axis_index("tensor") * local_rows
    full_query, full_key, full_value, full_out = (
        lax.all_gather(w_query, "dp", axis=0, tiled=True),
        lax.all_gather(w_key, "dp", axis=0, tiled=True),
        lax.all_gather(w_value, "dp", axis=0, tiled=True),
        lax.all_gather(w_out, "dp", axis=0, tiled=True),
    )

    def spread_out(weight):
        grouped = weight.reshape(clusters, holders, weight.shape[1], half_ff)
        return jnp.broadcast_to(grouped[None], (replicas,) + grouped.shape).reshape(
            dp_count, holders, weight.shape[1], half_ff
        )

    local_gate, local_up, local_down = (
        lax.all_to_all(spread_out(w_gate), "dp", split_axis=0, concat_axis=2, tiled=True),
        lax.all_to_all(spread_out(w_up), "dp", split_axis=0, concat_axis=2, tiled=True),
        lax.all_to_all(spread_out(w_down), "dp", split_axis=0, concat_axis=2, tiled=True),
    )
    local_gate = local_gate.reshape(holders, model_width, half_ff)
    local_up = local_up.reshape(holders, model_width, half_ff)
    local_down = local_down.reshape(holders, model_width, half_ff)
    tokens_f32 = tokens.astype(jnp.float32)
    position, allowed = seq_layout(lengths[0], row_count)
    cosine, sine_table = rope_tables(position, HEAD_DIM)
    unit_first, scale_first, normed_first = norm_forward(tokens_f32, attn_gain)
    wide_first = spread_rows(normed_first)
    query_heads = rotate(
        jnp.dot(wide_first, full_query, preferred_element_type=jnp.float32).reshape(
            row_count, heads_here, HEAD_DIM
        ),
        cosine,
        sine_table,
    ).astype(jnp.bfloat16)
    key_heads = rotate(
        jnp.dot(wide_first, full_key, preferred_element_type=jnp.float32).reshape(
            row_count, kv_here, HEAD_DIM
        ),
        cosine,
        sine_table,
    ).astype(jnp.bfloat16)
    value_heads = (
        jnp.dot(wide_first, full_value, preferred_element_type=jnp.float32)
        .astype(jnp.bfloat16)
        .reshape(row_count, kv_here, HEAD_DIM)
    )
    mixed_out, log_total = attend(query_heads, key_heads, value_heads, allowed)
    hidden = tokens_f32 + residual_scale * narrow(
        jnp.dot(mixed_out, full_out.T, preferred_element_type=jnp.float32)
    )
    unit_second, scale_second, normed_second = norm_forward(hidden, ffn_gain)
    wide_second = spread_rows(normed_second)
    expert_ids = jnp.arange(EXPERTS, dtype=jnp.int32)
    picked = routes[:, :, None] == expert_ids[None, None, :]
    logits = jnp.dot(wide_second.astype(jnp.float32), w_router, precision=lax.Precision.HIGHEST)
    chosen = jnp.sum(jnp.where(picked, logits[:, None, :], 0.0), axis=2)
    gate_probs = jax.nn.softmax(chosen, axis=1)
    flat_ids = routes.reshape(-1)
    onehot = (flat_ids[:, None] == expert_ids[None, :]).astype(jnp.int32)
    ordinal = jnp.sum((jnp.cumsum(onehot, axis=0) - 1) * onehot, axis=1)
    target = ordinal % replicas * clusters + flat_ids // holders
    slot_index = (target * holders + flat_ids % holders) * capacity + ordinal // replicas
    token_of = jnp.arange(row_count * TOPK, dtype=jnp.int32) // TOPK
    slot_count = dp_count * holders * capacity

    def pack_rows(route_rows):
        boxes = jnp.zeros((slot_count, model_width), jnp.bfloat16).at[slot_index].set(route_rows)
        return boxes.reshape(dp_count, holders * capacity, model_width)

    def unpack(boxes):
        return boxes.reshape(slot_count, model_width)[slot_index].reshape(
            row_count, TOPK, model_width
        )

    outgoing = pack_rows(wide_second[token_of])
    arrived = lax.all_to_all(outgoing, "dp", split_axis=0, concat_axis=0, tiled=True).reshape(
        dp_count, holders, capacity, model_width
    )
    gate_pre = jnp.einsum("secd,edf->secf", arrived, local_gate, preferred_element_type=jnp.float32)
    up_pre = jnp.einsum("secd,edf->secf", arrived, local_up, preferred_element_type=jnp.float32)
    inner_act = (gate_pre * jax.nn.sigmoid(gate_pre) * up_pre).astype(jnp.bfloat16)
    produced = jnp.einsum(
        "secf,edf->secd", inner_act, local_down, preferred_element_type=jnp.float32
    ).astype(jnp.bfloat16)
    routed = unpack(
        lax.all_to_all(
            produced.reshape(dp_count, holders * capacity, model_width),
            "dp",
            split_axis=0,
            concat_axis=0,
            tiled=True,
        )
    )
    moe_part = jnp.sum(gate_probs[:, :, None] * routed, axis=1)
    block_rows = (hidden + residual_scale * narrow(moe_part)).astype(jnp.bfloat16)
    out_f32 = out_grad.astype(jnp.float32)
    moe_grad = spread_rows((residual_scale * out_f32).astype(jnp.bfloat16)).astype(jnp.float32)
    gate_part = jnp.sum(moe_grad[:, None, :] * routed, axis=2)
    route_grad = (gate_probs[:, :, None] * moe_grad[:, None, :]).astype(jnp.bfloat16)
    grad_boxes = pack_rows(route_grad.reshape(row_count * TOPK, model_width))
    rows_again, grad_arrived = (
        lax.all_to_all(outgoing, "dp", split_axis=0, concat_axis=0, tiled=True),
        lax.all_to_all(grad_boxes, "dp", split_axis=0, concat_axis=0, tiled=True),
    )
    rows_again = rows_again.reshape(dp_count, holders, capacity, model_width)
    gate_pre = jnp.einsum(
        "secd,edf->secf", rows_again, local_gate, preferred_element_type=jnp.float32
    )
    up_pre = jnp.einsum("secd,edf->secf", rows_again, local_up, preferred_element_type=jnp.float32)
    grad_arrived = grad_arrived.reshape(dp_count, holders, capacity, model_width)
    sigmoid_gate = jax.nn.sigmoid(gate_pre)
    activated = gate_pre * sigmoid_gate
    inner_grad = jnp.einsum(
        "secd,edf->secf", grad_arrived, local_down, preferred_element_type=jnp.float32
    )
    gate_pre_grad = (
        inner_grad * up_pre * sigmoid_gate * (1.0 + gate_pre * (1.0 - sigmoid_gate))
    ).astype(jnp.bfloat16)
    up_pre_grad = (inner_grad * activated).astype(jnp.bfloat16)
    inner_again = (activated * up_pre).astype(jnp.bfloat16)
    rows_back = jnp.einsum(
        "secf,edf->secd", gate_pre_grad, local_gate, preferred_element_type=jnp.float32
    )
    rows_back = (
        rows_back
        + jnp.einsum("secf,edf->secd", up_pre_grad, local_up, preferred_element_type=jnp.float32)
    ).astype(jnp.bfloat16)
    gate_w_grad = jnp.einsum(
        "secd,secf->edf", rows_again, gate_pre_grad, preferred_element_type=jnp.float32
    )
    up_w_grad = jnp.einsum(
        "secd,secf->edf", rows_again, up_pre_grad, preferred_element_type=jnp.float32
    )
    down_w_grad = jnp.einsum(
        "secd,secf->edf", grad_arrived, inner_again, preferred_element_type=jnp.float32
    )
    routed_back = unpack(
        lax.all_to_all(
            rows_back.reshape(dp_count, holders * capacity, model_width),
            "dp",
            split_axis=0,
            concat_axis=0,
            tiled=True,
        )
    )
    second_part = jnp.sum(routed_back.astype(jnp.float32), axis=1)
    expert_back, gate_grad = (
        lax.psum_scatter(second_part, "tensor", scatter_dimension=0, tiled=True),
        lax.psum_scatter(gate_part, "tensor", scatter_dimension=0, tiled=True),
    )
    home_gate, home_up, home_down = (
        lax.all_to_all(
            gate_w_grad[None].astype(jnp.bfloat16), "dp", split_axis=2, concat_axis=0, tiled=True
        ).astype(jnp.float32),
        lax.all_to_all(
            up_w_grad[None].astype(jnp.bfloat16), "dp", split_axis=2, concat_axis=0, tiled=True
        ).astype(jnp.float32),
        lax.all_to_all(
            down_w_grad[None].astype(jnp.bfloat16), "dp", split_axis=2, concat_axis=0, tiled=True
        ).astype(jnp.float32),
    )

    def fold_home(gradient):
        return jnp.sum(
            gradient.reshape(replicas, clusters * holders, gradient.shape[2], half_ff), axis=0
        )

    gates_own = lax.dynamic_slice_in_dim(gate_probs, own_row, local_rows, 0)
    picked_own = lax.dynamic_slice_in_dim(picked, own_row, local_rows, 0)
    chosen_grad = gates_own * (gate_grad - jnp.sum(gates_own * gate_grad, axis=1, keepdims=True))
    logits_grad = jnp.sum(jnp.where(picked_own, chosen_grad[:, :, None], 0.0), axis=1)
    second_grad = expert_back + jnp.dot(logits_grad, w_router.T, precision=lax.Precision.HIGHEST)
    router_grad = jnp.dot(
        normed_second.astype(jnp.float32).T, logits_grad, precision=lax.Precision.HIGHEST
    )
    hidden_back, ffn_gain_grad = norm_backward(second_grad, unit_second, scale_second, ffn_gain)
    hidden_grad = out_f32 + hidden_back
    attn_grad = spread_rows((residual_scale * hidden_grad).astype(jnp.bfloat16))
    mixed_grad = jnp.dot(attn_grad, full_out, preferred_element_type=jnp.float32).astype(
        jnp.bfloat16
    )
    out_w_grad = jnp.dot(attn_grad.T, mixed_out, preferred_element_type=jnp.float32)
    dquery, key_grad, dvalues = attend_back(
        query_heads, key_heads, value_heads, allowed, log_total, mixed_grad
    )
    query_grad = (
        unrotate(dquery, cosine, sine_table)
        .astype(jnp.bfloat16)
        .reshape(row_count, heads_here * HEAD_DIM)
    )
    keys_grad = (
        unrotate(key_grad, cosine, sine_table)
        .astype(jnp.bfloat16)
        .reshape(row_count, kv_here * HEAD_DIM)
    )
    value_grad = dvalues.astype(jnp.bfloat16).reshape(row_count, kv_here * HEAD_DIM)
    query_w_grad = jnp.dot(wide_first.T, query_grad, preferred_element_type=jnp.float32)
    key_w_grad = jnp.dot(wide_first.T, keys_grad, preferred_element_type=jnp.float32)
    value_w_grad = jnp.dot(wide_first.T, value_grad, preferred_element_type=jnp.float32)
    first_part = jnp.dot(query_grad, full_query.T, preferred_element_type=jnp.float32)
    first_part = first_part + jnp.dot(keys_grad, full_key.T, preferred_element_type=jnp.float32)
    first_part = first_part + jnp.dot(value_grad, full_value.T, preferred_element_type=jnp.float32)
    first_grad = narrow(first_part)
    tokens_back, attn_gain_grad = norm_backward(first_grad, unit_first, scale_first, attn_gain)
    tokens_grad = hidden_grad + tokens_back
    query_total, key_total, value_total, out_total = (
        lax.psum_scatter(query_w_grad, "dp", scatter_dimension=0, tiled=True),
        lax.psum_scatter(key_w_grad, "dp", scatter_dimension=0, tiled=True),
        lax.psum_scatter(value_w_grad, "dp", scatter_dimension=0, tiled=True),
        lax.psum_scatter(out_w_grad, "dp", scatter_dimension=0, tiled=True),
    )
    attn_gain_total, ffn_gain_total, router_total = lax.psum(
        (attn_gain_grad, ffn_gain_grad, router_grad), ("dp", "tensor")
    )
    return (
        block_rows,
        tokens_grad,
        attn_gain_total,
        query_total,
        key_total,
        value_total,
        out_total,
        ffn_gain_total,
        router_total,
        fold_home(home_gate),
        fold_home(home_up),
        fold_home(home_down),
    )


def solution(mesh):
    placed = (
        P(("dp", "tensor"), None),
        P(("dp", "tensor"), None),
        P("dp", None),
        P("dp", None),
        P(),
        P("dp", "tensor"),
        P("dp", "tensor"),
        P("dp", "tensor"),
        P("dp", "tensor"),
        P(),
        P(),
        P(None, "dp", "tensor"),
        P(None, "dp", "tensor"),
        P(None, "dp", "tensor"),
    )
    return jax.shard_map(
        local,
        mesh=mesh,
        in_specs=placed,
        out_specs=(
            P(("dp", "tensor"), None),
            P(("dp", "tensor"), None),
            P(),
            P("dp", "tensor"),
            P("dp", "tensor"),
            P("dp", "tensor"),
            P("dp", "tensor"),
            P(),
            P(),
            P(None, "dp", "tensor"),
            P(None, "dp", "tensor"),
            P(None, "dp", "tensor"),
        ),
        check_vma=False,
    )
```

profile of v0, /device:TPU:0, one launch (start us, length us, event | category | flops | bytes accessed | tf_op | source)
XLA Modules:
  0.0 947.0 jit_solution(10804342848170148247)
XLA Ops:
  7.9 7.4 all-to-all-start.1
  19.8 6.5 all_gather.24
  26.6 26.4 %all_gather.26 = bf16[1024,256]{1,0:T(8,128)(2,1)S(1)} all-gather(bf16[64,256]{1,0:T(8,128)(2,1)} %param.20), channel_id=1, replica_groups=mesh['dp'=16,'tensor'=2] {'dp'}, dimensions={0}, use_global_device_ids=true | all-gather | bytes 557056 | tf_op jit(solution)/shard_map/all_gather | solution.py:155
  54.1 24.0 %all_gather.25 = bf16[1024,256]{1,0:T(8,128)(2,1)S(1)} all-gather(bf16[64,256]{1,0:T(8,128)(2,1)S(1)} %copy-done.50), channel_id=1, replica_groups=mesh['dp'=16,'tensor'=2] {'dp'}, dimensions={0}, use_global_device_ids=true | all-gather | bytes 557056 | tf_op jit(solution)/shard_map/all_gather | solution.py:156
  79.2 3.7 all-to-all-start.2
  84.1 1.8 fusion.73
  87.3 21.9 %all-to-all-done.2 = bf16[16,2,64,256]{3,2,1,0:T(8,128)(2,1)S(1)} async-done(((bf16[16,2,64,256]{3,2,1,0:T(8,128)(2,1)}), bf16[16,2,64,256]{3,2,1,0:T(8,128)(2,1)S(1)}, u32[]{:S(2)}, u32[]{:S(2)}) %all-to-all-start.2) | async-done | bytes 1048608 | tf_op jit(solution)/shard_map/all_to_all | solution.py:168
  109.3 7.0 all-to-all-start.3
  116.3 2.5 fusion.74
  118.9 9.0 reduce-window.11
  128.5 7.5 reduce-scatter.12.cloned.1.call-done
  138.6 5.8 all_gather.29
  144.3 14.9 %scatter_custom_fusion = bf16[1536,1024]{1,0:T(8,128)(2,1)} fusion(s32[1024]{0:T(1024)S(1)} %bitcast.303, bf16[128,1024]{1,0:T(8,128)(2,1)S(1)} %all_gather.29, s32[1024]{0:T(1024)S(1)} %broadcast_clamp_fusion.1, bf16[]{:T(256)} %constant.101.clone.1), kind=kCustom, calls=%fused_computation.28 | custom fusion | bytes 3145730 | tf_op jit(solution)/shard_map/scatter | solution.py:218
  159.3 5.8 all-to-all-start
  165.1 6.4 all_gather.30
  172.3 7.9 scatter_custom_fusion.1
  180.1 44.2 %all-to-all-done = bf16[16,96,1024]{2,1,0:T(8,128)(2,1)} async-done(((bf16[16,96,1024]{2,1,0:T(8,128)(2,1)}), bf16[16,96,1024]{2,1,0:T(8,128)(2,1)}, u32[]{:S(2)}, u32[]{:S(2)}) %all-to-all-start) | async-done | bytes 3145760 | tf_op jit(solution)/shard_map/all_to_all | solution.py:227
  224.4 15.5 %all-to-all-start.5 = ((bf16[16,96,1024]{2,1,0:T(8,128)(2,1)}), bf16[16,96,1024]{2,1,0:T(8,128)(2,1)}, u32[]{:S(2)}, u32[]{:S(2)}) async-start(bf16[16,96,1024]{2,1,0:T(8,128)(2,1)} %bitcast.49), calls=%async_computation.7 | async-start | bytes 6291456 | tf_op jit(solution)/shard_map/all_to_all | solution.py:254
  240.1 2.0 copy.159
  242.0 2.9 fusion.6
  244.9 4.0 fusion.8
  249.0 50.2 %all-to-all-done.5 = bf16[16,96,1024]{2,1,0:T(8,128)(2,1)} async-done(((bf16[16,96,1024]{2,1,0:T(8,128)(2,1)}), bf16[16,96,1024]{2,1,0:T(8,128)(2,1)}, u32[]{:S(2)}, u32[]{:S(2)}) %all-to-all-start.5) | async-done | bytes 3145760 | tf_op jit(solution)/shard_map/all_to_all | solution.py:254
  299.2 5.1 fusion.19
  305.3 2.2 copy.160
  307.5 15.6 %all-to-all-start.4 = ((bf16[16,96,1024]{2,1,0:T(8,128)(2,1)}), bf16[16,96,1024]{2,1,0:T(8,128)(2,1)S(1)}, u32[]{:S(2)}, u32[]{:S(2)}) async-start(bf16[16,96,1024]{2,1,0:T(8,128)(2,1)} %bitcast.260), calls=%async_computation.5 | async-start | bytes 6291456 | tf_op jit(solution)/shard_map/all_to_all | solution.py:237
  323.2 2.6 fusion.76
  326.8 2.1 copy.163
  328.9 53.4 %all-to-all-done.4 = bf16[16,96,1024]{2,1,0:T(8,128)(2,1)S(1)} async-done(((bf16[16,96,1024]{2,1,0:T(8,128)(2,1)}), bf16[16,96,1024]{2,1,0:T(8,128)(2,1)S(1)}, u32[]{:S(2)}, u32[]{:S(2)}) %all-to-all-start.4) | async-done | bytes 3145760 | tf_op jit(solution)/shard_map/all_to_all | solution.py:237
  382.3 1.7 copy-done.1
  384.0 15.4 %all-to-all-start.6 = ((bf16[16,96,1024]{2,1,0:T(8,128)(2,1)}), bf16[16,96,1024]{2,1,0:T(8,128)(2,1)S(1)}, u32[]{:S(2)}, u32[]{:S(2)}) async-start(bf16[16,96,1024]{2,1,0:T(8,128)(2,1)} %bitcast.259), calls=%async_computation.8 | async-start | bytes 6291456 | tf_op jit(solution)/shard_map/all_to_all | solution.py:289
  399.5 8.3 gather_fusion
  407.8 4.2 fusion.1
  412.1 46.5 %all-to-all-done.6 = bf16[16,96,1024]{2,1,0:T(8,128)(2,1)S(1)} async-done(((bf16[16,96,1024]{2,1,0:T(8,128)(2,1)}), bf16[16,96,1024]{2,1,0:T(8,128)(2,1)S(1)}, u32[]{:S(2)}, u32[]{:S(2)}) %all-to-all-start.6) | async-done | bytes 3145760 | tf_op jit(solution)/shard_map/all_to_all | solution.py:289
  458.7 5.3 gather_fusion.1
  464.0 3.9 convert_reduce_fusion
  469.2 23.4 %reduce-scatter.16.cloned.1.call-done = f32[64,1024]{1,0:T(8,128)} async-done(((f32[128,1024]{1,0:T(8,128)}), f32[64,1024]{1,0:T(8,128)}) %reduce-scatter.16.cloned.1.call-update) | async-done | bytes 262160 | tf_op jit(solution)/shard_map/reduce_scatter | solution.py:299
  492.6 2.0 multiply_reduce_fusion.1
  495.4 5.7 all_gather.31
  514.8 3.4 fusion.29
  518.2 2.0 copy.176
  520.3 5.6 all-to-all-start.9
  525.9 1.8 fusion.79
  527.8 3.4 fusion.27
  531.2 2.0 copy.170
  533.3 15.5 %all-to-all-done.9 = bf16[1,2,1024,256]{3,1,0,2:T(2,128)(2,1)S(1)} async-done(((bf16[1,2,1024,256]{3,1,0,2:T(2,128)(2,1)}), bf16[1,2,1024,256]{3,1,0,2:T(2,128)(2,1)S(1)}, u32[]{:S(2)}, u32[]{:S(2)}) %all-to-all-start.9) | async-done | bytes 1048608 | tf_op jit(solution)/shard_map/all_to_all | solution.py:309
  548.8 6.8 all-to-all-start.7
  555.6 1.8 fusion.82
  557.4 3.4 fusion.28
  560.9 2.0 copy.173
  562.9 15.9 %all-to-all-done.7 = bf16[1,2,1024,256]{3,1,0,2:T(2,128)(2,1)S(1)} async-done(((bf16[1,2,1024,256]{3,1,0,2:T(2,128)(2,1)}), bf16[1,2,1024,256]{3,1,0,2:T(2,128)(2,1)S(1)}, u32[]{:S(2)}, u32[]{:S(2)}) %all-to-all-start.7) | async-done | bytes 1048608 | tf_op jit(solution)/shard_map/all_to_all | solution.py:303
  578.9 7.2 all-to-all-start.8
  586.9 1.6 copy.177
  589.4 1.6 copy.171
  591.0 18.3 %all-to-all-done.8 = bf16[1,2,1024,256]{3,1,0,2:T(2,128)(2,1)} async-done(((bf16[1,2,1024,256]{3,1,0,2:T(2,128)(2,1)}), bf16[1,2,1024,256]{3,1,0,2:T(2,128)(2,1)}, u32[]{:S(2)}, u32[]{:S(2)}) %all-to-all-start.8) | async-done | bytes 1048608 | tf_op jit(solution)/shard_map/all_to_all | solution.py:306
  609.4 2.2 convert_bitcast_fusion.2
  611.6 1.6 copy.174
  614.4 42.2 %all-reduce = (f32[1024]{0:T(1024)}, f32[1024]{0:T(1024)}) all-reduce(f32[1024]{0:T(1024)S(1)} %get-tuple-element.16, f32[1024]{0:T(1024)S(1)} %copy-done.51), channel_id=1, replica_groups=mesh['dp'=16,'tensor'=2] {'dp','tensor'}, use_global_device_ids=true, to_apply=%region_29.30 | all-reduce | flops 2048 | bytes 16384 | tf_op jit(solution)/shard_map/psum | solution.py:363
  656.6 2.0 fusion.47
  658.6 27.9 %all-reduce.3.cloned.1.call-done = f32[1024,32]{0,1:T(8,128)} async-done(((f32[1024,32]{0,1:T(8,128)}), f32[1024,32]{0,1:T(8,128)}) %all-reduce.3.cloned.1.call-update) | async-done | bytes 131088 | tf_op jit(solution)/shard_map/psum | solution.py:363
  686.5 60.8 %reduce-scatter.22.cloned.1.call-done = f32[64,256]{1,0:T(8,128)} async-done(((f32[1024,256]{1,0:T(8,128)}), f32[64,256]{1,0:T(8,128)}) %reduce-scatter.22.cloned.1.call-update) | async-done | bytes 65552 | tf_op jit(solution)/shard_map/reduce_scatter | solution.py:359
  747.3 60.7 %reduce-scatter.24.cloned.1.call-done = f32[64,256]{1,0:T(8,128)} async-done(((f32[1024,256]{1,0:T(8,128)}), f32[64,256]{1,0:T(8,128)}) %reduce-scatter.24.cloned.1.call-update) | async-done | bytes 65552 | tf_op jit(solution)/shard_map/reduce_scatter | solution.py:360
  808.0 65.2 %reduce-scatter.20.cloned.1.call-done = f32[64,512]{1,0:T(8,128)} async-done(((f32[1024,512]{1,0:T(8,128)}), f32[64,512]{1,0:T(8,128)}) %reduce-scatter.20.cloned.1.call-update) | async-done | bytes 131088 | tf_op jit(solution)/shard_map/reduce_scatter | solution.py:358
  873.2 64.9 %reduce-scatter.26.cloned.1.call-done = f32[64,512]{1,0:T(8,128)} async-done(((f32[1024,512]{1,0:T(8,128)}), f32[64,512]{1,0:T(8,128)}) %reduce-scatter.26.cloned.1.call-update) | async-done | bytes 131088 | tf_op jit(solution)/shard_map/reduce_scatter | solution.py:361
  938.1 1.6 copy.210
  (233 shorter events, 34.7 us)
Async XLA Ops:
  7.2 164.4 %copy-start = (f32[1024,32]{0,1:T(8,128)S(1)}, f32[1024,32]{0,1:T(8,128)}, u32[]{:S(2)}) copy-start(f32[1024,32]{0,1:T(8,128)} %param.24) | copy-start | bytes 393220
  7.2 46.9 %copy-start.50 = (bf16[64,256]{1,0:T(8,128)(2,1)S(1)}, bf16[64,256]{1,0:T(8,128)(2,1)}, u32[]{:S(2)}) copy-start(bf16[64,256]{1,0:T(8,128)(2,1)} %param.21) | copy-start | bytes 98308
  7.2 76.9 %all-gather.3.cloned.1.call-start = ((), (), s32[]{:S(2)}) async-start(), calls=%async_computation.19 | async-start | bytes 1114112 | tf_op jit(solution)/shard_map/all_gather | solution.py:154
  7.9 71.3 %all-to-all-start.1 = ((bf16[16,2,64,256]{3,2,1,0:T(8,128)(2,1)}), bf16[16,2,64,256]{3,2,1,0:T(8,128)(2,1)S(1)}, u32[]{:S(2)}, u32[]{:S(2)}) async-start(bf16[16,2,64,256]{3,2,1,0:T(8,128)(2,1)} %bitcast.283), calls=%async_computation.2 | async-start | bytes 2097152 | tf_op jit(solution)/shard_map/all_to_all | solution.py:167
  15.3 67.6 %copy-start.49 = (s32[128,8]{0,1:T(8,128)S(1)}, s32[128,8]{0,1:T(8,128)}, u32[]{:S(2)}) copy-start(s32[128,8]{0,1:T(8,128)} %param.17) | copy-start | bytes 12292
  15.4 101.0 %all-gather.5.cloned.1.call-start = ((), (), s32[]{:S(2)}) async-start(), calls=%async_computation.20 | async-start | bytes 1114112 | tf_op jit(solution)/shard_map/all_gather | solution.py:157
  18.7 35.4 %copy-start.55 = (f32[64]{0:T(128)}, f32[64]{0:T(128)S(1)}, u32[]{:S(2)}) copy-start(f32[64]{0:T(128)S(1)} %add_rsqrt_fusion.1) | copy-start | bytes 772
  79.2 30.0 %all-to-all-start.2 = ((bf16[16,2,64,256]{3,2,1,0:T(8,128)(2,1)}), bf16[16,2,64,256]{3,2,1,0:T(8,128)(2,1)S(1)}, u32[]{:S(2)}, u32[]{:S(2)}) async-start(bf16[16,2,64,256]{3,2,1,0:T(8,128)(2,1)} %bitcast.284), calls=%async_computation.3 | async-start | bytes 2097152 | tf_op jit(solution)/shard_map/all_to_all | solution.py:168
  82.9 3.5 copy-start.29
  83.4 25.8 %copy-start.36 = (bf16[128,256]{0,1:T(8,128)(2,1)}, bf16[128,256]{0,1:T(8,128)(2,1)S(1)}, u32[]{:S(2)}) copy-start(bf16[128,256]{0,1:T(8,128)(2,1)S(1)} %copy.144) | copy-start | bytes 196612
  86.4 32.4 %copy-start.44 = (f32[1,8,128]{2,1,0:T(8,128)}, f32[1,8,128]{2,1,0:T(8,128)S(1)}, u32[]{:S(2)}) copy-start(f32[1,8,128]{2,1,0:T(8,128)S(1)} %log_add_fusion) | copy-start | bytes 12292
  87.1 48.9 %copy-start.16 = (bf16[64,1024]{1,0:T(8,128)(2,1)S(1)}, bf16[64,1024]{1,0:T(8,128)(2,1)}, u32[]{:S(2)}) copy-start(bf16[64,1024]{1,0:T(8,128)(2,1)} %param.14) | copy-start | bytes 393220
  87.3 31.6 %copy-start.24 = (bf16[4,64,2,128]{3,1,2,0:T(8,128)(2,1)}, bf16[4,64,2,128]{3,1,2,0:T(8,128)(2,1)S(1)}, u32[]{:S(2)}) copy-start(bf16[4,64,2,128]{3,1,2,0:T(8,128)(2,1)S(1)} %convolution_convert_fusion.1) | copy-start | bytes 393220
  87.3 50.5 %copy-start.45 = (f32[1024]{0:T(1024)S(1)}, f32[1024]{0:T(1024)}, u32[]{:S(2)}) copy-start(f32[1024]{0:T(1024)} %param.23) | copy-start | bytes 12292
  109.3 50.0 %all-to-all-start.3 = ((bf16[16,2,64,256]{3,2,1,0:T(8,128)(2,1)}), bf16[16,2,64,256]{3,2,1,0:T(8,128)(2,1)}, u32[]{:S(2)}, u32[]{:S(2)}) async-start(bf16[16,2,64,256]{3,2,1,0:T(8,128)(2,1)} %bitcast.285), calls=%async_computation.4 | async-start | bytes 2097152 | tf_op jit(solution)/shard_map/all_to_all | solution.py:169
  116.3 19.7 %reduce-scatter.12.cloned.1.call-start = ((), (), s32[]{:S(2)}) async-start(), calls=%async_computation.21 | async-start | bytes 786432 | tf_op jit(solution)/shard_map/reduce_scatter | solution.py:122
  137.1 22.2 %copy-start.52 = (f32[64]{0:T(128)}, f32[64]{0:T(128)S(1)}, u32[]{:S(2)}) copy-start(f32[64]{0:T(128)S(1)} %add_rsqrt_fusion) | copy-start | bytes 772
  159.3 5.8 copy-start.26
  159.3 65.1 %all-to-all-start = ((bf16[16,96,1024]{2,1,0:T(8,128)(2,1)}), bf16[16,96,1024]{2,1,0:T(8,128)(2,1)}, u32[]{:S(2)}, u32[]{:S(2)}) async-start(bf16[16,96,1024]{2,1,0:T(8,128)(2,1)} %bitcast.22), calls=%async_computation.1 | async-start | bytes 6291456 | tf_op jit(solution)/shard_map/all_to_all | solution.py:227
  171.6 52.8 %copy-start.6 = (f32[128,1024]{1,0:T(8,128)}, f32[128,1024]{1,0:T(8,128)S(1)}, u32[]{:S(2)}) copy-start(f32[128,1024]{1,0:T(8,128)S(1)} %convert_element_type.207) | copy-start | bytes 1572868
  172.2 52.2 %copy-start.35 = (f32[128,8]{1,0:T(8,128)}, f32[128,8]{1,0:T(8,128)S(1)}, u32[]{:S(2)}) copy-start(f32[128,8]{1,0:T(8,128)S(1)} %copy.149) | copy-start | bytes 12292
  224.4 74.8 %all-to-all-start.5 = ((bf16[16,96,1024]{2,1,0:T(8,128)(2,1)}), bf16[16,96,1024]{2,1,0:T(8,128)(2,1)}, u32[]{:S(2)}, u32[]{:S(2)}) async-start(bf16[16,96,1024]{2,1,0:T(8,128)(2,1)} %bitcast.49), calls=%async_computation.7 | async-start | bytes 6291456 | tf_op jit(solution)/shard_map/all_to_all | solution.py:254
  240.0 5.0 copy-start.15
  240.0 4.9 copy-start.13
  307.5 74.9 %all-to-all-start.4 = ((bf16[16,96,1024]{2,1,0:T(8,128)(2,1)}), bf16[16,96,1024]{2,1,0:T(8,128)(2,1)S(1)}, u32[]{:S(2)}, u32[]{:S(2)}) async-start(bf16[16,96,1024]{2,1,0:T(8,128)(2,1)} %bitcast.260), calls=%async_computation.5 | async-start | bytes 6291456 | tf_op jit(solution)/shard_map/all_to_all | solution.py:237
  384.0 74.7 %all-to-all-start.6 = ((bf16[16,96,1024]{2,1,0:T(8,128)(2,1)}), bf16[16,96,1024]{2,1,0:T(8,128)(2,1)S(1)}, u32[]{:S(2)}, u32[]{:S(2)}) async-start(bf16[16,96,1024]{2,1,0:T(8,128)(2,1)} %bitcast.259), calls=%async_computation.8 | async-start | bytes 6291456 | tf_op jit(solution)/shard_map/all_to_all | solution.py:289
  399.4 68.7 %reduce-scatter.28.cloned.1.call-start = ((), (), s32[]{:S(2)}) async-start(), calls=%async_computation.30 | async-start | bytes 98304
  412.1 80.5 %reduce-scatter.16.cloned.1.call-start = ((), (), s32[]{:S(2)}) async-start(), calls=%async_computation.23 | async-start | bytes 786432 | tf_op jit(solution)/shard_map/reduce_scatter | solution.py:299
  464.0 28.6 %copy-start.5 = (f32[64,1024]{1,0:T(8,128)S(1)}, f32[64,1024]{1,0:T(8,128)}, u32[]{:S(2)}) copy-start(f32[64,1024]{1,0:T(8,128)} %copy-done.4) | copy-start | bytes 786436
  464.0 28.6 %copy-start.46 = (f32[1024]{0:T(1024)S(1)}, f32[1024]{0:T(1024)}, u32[]{:S(2)}) copy-start(f32[1024]{0:T(1024)} %param.23) | copy-start | bytes 12292
  464.0 28.6 %copy-start.53 = (f32[64]{0:T(128)S(1)}, f32[64]{0:T(128)}, u32[]{:S(2)}) copy-start(f32[64]{0:T(128)} %copy-done.52) | copy-start | bytes 772
  464.0 31.2 %copy-start.27 = (bf16[64,1024]{1,0:T(8,128)(2,1)S(1)}, bf16[64,1024]{1,0:T(8,128)(2,1)}, u32[]{:S(2)}) copy-start(bf16[64,1024]{1,0:T(8,128)(2,1)} %param.15) | copy-start | bytes 393220
  464.0 37.1 %copy-start.12 = (bf16[1024,512]{1,0:T(8,128)(2,1)S(1)}, bf16[1024,512]{1,0:T(8,128)(2,1)}, u32[]{:S(2)}) copy-start(bf16[1024,512]{1,0:T(8,128)(2,1)} %all-gather.5.cloned.1.call-done) | copy-start | bytes 3145732
  464.0 39.1 %copy-start.3 = (f32[4,2,128,128]{2,3,1,0:T(8,128)S(1)}, f32[4,2,128,128]{2,3,1,0:T(8,128)}, u32[]{:S(2)}) copy-start(f32[4,2,128,128]{2,3,1,0:T(8,128)} %copy-done.2) | copy-start | bytes 1572868
  468.0 145.2 %reduce-scatter.18.cloned.1.call-start = ((), (), s32[]{:S(2)}) async-start(), calls=%async_computation.24 | async-start | bytes 786432 | tf_op jit(solution)/shard_map/reduce_scatter | solution.py:122
  494.6 11.5 %copy-start.23 = (bf16[128,4,2,64]{0,3,2,1:T(8,128)(2,1)S(1)}, bf16[128,4,2,64]{0,3,2,1:T(8,128)(2,1)}, u32[]{:S(2)}) copy-start(bf16[128,4,2,64]{0,3,2,1:T(8,128)(2,1)} %copy-done.22) | copy-start | bytes 393220
  501.1 6.7 copy-start.18
  501.1 6.3 copy-start.10
  502.1 5.7 copy-start.30
  502.1 5.7 copy-start.43
  503.1 4.7 copy-start.8
  504.1 4.1 copy-start.39
  505.3 3.2 copy-start.42
  508.6 4.8 copy-start.40
  509.9 4.9 copy-start.32
  509.9 146.6 %reduce-scatter.14.cloned.1.call-start = ((), (), s32[]{:S(2)}) async-start(), calls=%async_computation.22 | async-start | bytes 786432 | tf_op jit(solution)/shard_map/reduce_scatter | solution.py:122
  510.7 175.8 %all-reduce.3.cloned.1.call-start = ((), (), s32[]{:S(2)}) async-start(), calls=%async_computation.29 | async-start | bytes 262144 | tf_op jit(solution)/shard_map/psum | solution.py:363
  511.6 235.7 %reduce-scatter.22.cloned.1.call-start = ((), (), s32[]{:S(2)}) async-start(), calls=%async_computation.26 | async-start | bytes 1114112 | tf_op jit(solution)/shard_map/reduce_scatter | solution.py:359
  513.1 295.0 %reduce-scatter.24.cloned.1.call-start = ((), (), s32[]{:S(2)}) async-start(), calls=%async_computation.27 | async-start | bytes 1114112 | tf_op jit(solution)/shard_map/reduce_scatter | solution.py:360
  520.3 28.5 %all-to-all-start.9 = ((bf16[1,2,1024,256]{3,1,0,2:T(2,128)(2,1)}), bf16[1,2,1024,256]{3,1,0,2:T(2,128)(2,1)S(1)}, u32[]{:S(2)}, u32[]{:S(2)}) async-start(bf16[1,2,1024,256]{3,1,0,2:T(2,128)(2,1)} %copy.176), calls=%async_computation.17 | async-start | bytes 2097152 | tf_op jit(solution)/shard_map/all_to_all | solution.py:309
  525.9 347.3 %reduce-scatter.20.cloned.1.call-start = ((), (), s32[]{:S(2)}) async-start(), calls=%async_computation.25 | async-start | bytes 2228224 | tf_op jit(solution)/shard_map/reduce_scatter | solution.py:358
  531.2 24.4 %copy-start.19 = (bf16[128,1024]{1,0:T(8,128)(2,1)S(1)}, bf16[128,1024]{1,0:T(8,128)(2,1)}, u32[]{:S(2)}) copy-start(bf16[128,1024]{1,0:T(8,128)(2,1)} %copy-done.18) | copy-start | bytes 786436
  531.2 24.4 %copy-start.25 = (bf16[4,64,2,128]{3,1,2,0:T(8,128)(2,1)S(1)}, bf16[4,64,2,128]{3,1,2,0:T(8,128)(2,1)}, u32[]{:S(2)}) copy-start(bf16[4,64,2,128]{3,1,2,0:T(8,128)(2,1)} %copy-done.24) | copy-start | bytes 393220
  548.8 30.1 %all-to-all-start.7 = ((bf16[1,2,1024,256]{3,1,0,2:T(2,128)(2,1)}), bf16[1,2,1024,256]{3,1,0,2:T(2,128)(2,1)S(1)}, u32[]{:S(2)}, u32[]{:S(2)}) async-start(bf16[1,2,1024,256]{3,1,0,2:T(2,128)(2,1)} %copy.170), calls=%async_computation.15 | async-start | bytes 2097152 | tf_op jit(solution)/shard_map/all_to_all | solution.py:303
  555.6 382.6 %reduce-scatter.26.cloned.1.call-start = ((), (), s32[]{:S(2)}) async-start(), calls=%async_computation.28 | async-start | bytes 2228224 | tf_op jit(solution)/shard_map/reduce_scatter | solution.py:361
  578.9 30.4 %all-to-all-start.8 = ((bf16[1,2,1024,256]{3,1,0,2:T(2,128)(2,1)}), bf16[1,2,1024,256]{3,1,0,2:T(2,128)(2,1)}, u32[]{:S(2)}, u32[]{:S(2)}) async-start(bf16[1,2,1024,256]{3,1,0,2:T(2,128)(2,1)} %copy.173), calls=%async_computation.16 | async-start | bytes 2097152 | tf_op jit(solution)/shard_map/all_to_all | solution.py:306
  609.3 3.9 copy-start.17
  609.3 3.9 copy-start.48
  609.3 3.9 copy-start.56
  609.3 5.1 copy-start.51
  609.3 47.3 %copy-start.28 = (bf16[64,1024]{1,0:T(8,128)(2,1)S(1)}, bf16[64,1024]{1,0:T(8,128)(2,1)}, u32[]{:S(2)}) copy-start(bf16[64,1024]{1,0:T(8,128)(2,1)} %param.15) | copy-start | bytes 393220
  609.3 47.2 %copy-start.47 = (f32[1024]{0:T(1024)S(1)}, f32[1024]{0:T(1024)}, u32[]{:S(2)}) copy-start(f32[1024]{0:T(1024)} %param.23) | copy-start | bytes 12292
  609.3 47.2 %copy-start.54 = (f32[64]{0:T(128)S(1)}, f32[64]{0:T(128)}, u32[]{:S(2)}) copy-start(f32[64]{0:T(128)} %copy-done.52) | copy-start | bytes 772
  609.4 47.2 %copy-start.58 = (f32[64]{0:T(128)S(1)}, f32[64]{0:T(128)}, u32[]{:S(2)}) copy-start(f32[64]{0:T(128)} %copy-done.57) | copy-start | bytes 772
  (17 other events, 28.8 us)
Sparse Core Ops, SparseCore 0:
  10.2 47.2 all-gather.2
  59.7 43.3 all-gather.4
  119.9 16.0 reduce-scatter.11
  412.2 10.3 reduce-scatter.27
  468.1 24.4 reduce-scatter.15
  510.0 14.6 reduce-scatter.17
  527.0 14.6 reduce-scatter.13
  547.2 139.2 all-reduce.2
  690.7 56.5 reduce-scatter.21
  751.4 56.6 reduce-scatter.23
  812.3 60.8 reduce-scatter.19
  877.4 60.6 reduce-scatter.25
where the time goes:
time: 957 us; the launch traced here: 947 us
  waiting for transfers between devices  579 us (61%)
  blocking collectives  117 us (12%)
  starting transfers between devices  90.7 us (9%)
  local copies, waits for them, and re-layouts  56.6 us (6%)
  matrix products  48.2 us (5%)
  other arithmetic  39.9 us (4%)
  between operations  15.9 us (2%)
    reduce_scatter x1, waiting for transfers between devices, local(): lax.psum_scatter(query_w_grad, 'dp', scatter_dimension=0, tiled=True)  65.2 us
    reduce_scatter x1, waiting for transfers between devices, local(): lax.psum_scatter(out_w_grad, 'dp', scatter_dimension=0, tiled=True)  64.9 us
    reduce_scatter x1, waiting for transfers between devices, local(): lax.psum_scatter(key_w_grad, 'dp', scatter_dimension=0, tiled=True)  60.8 us
    reduce_scatter x1, waiting for transfers between devices, local(): lax.psum_scatter(value_w_grad, 'dp', scatter_dimension=0, tiled=True)  60.7 us
    all_to_all x1, waiting for transfers between devices, local(): lax.all_to_all(produced.reshape(dp_count, holders * capacity, model_width...  53.4 us
    all_to_all x1, waiting for transfers between devices, local(): lax.all_to_all(grad_boxes, 'dp', split_axis=0, concat_axis=0, tiled=True)  50.2 us
    all_to_all x1, waiting for transfers between devices, local(): lax.all_to_all(rows_back.reshape(dp_count, holders * capacity, model_widt...  46.5 us
    all_to_all x1, waiting for transfers between devices, local(): lax.all_to_all(outgoing, 'dp', split_axis=0, concat_axis=0, tiled=True)  44.2 us
  transfers between devices with their start and end apart: 22, of which 15 were waited for; matrix products, arithmetic and copies ran while one was open for 12% of the time, Pallas kernels for 0%

commit v1 on v0

v1 whole, which is shorter than its diff:
```python
import jax
import jax.numpy as jnp
from jax import lax
from jax.sharding import PartitionSpec as P

EXPERTS = 32
TOPK = 8
HEAD_DIM = 64


eps_norm = 1e-06
residual_scale = 0.22
score_scale = 0.015625
rope_base = 10000.0
masked_score = -1e30


def norm_forward(row_block, gain_vec):
    rscale = lax.rsqrt(jnp.mean(row_block * row_block, axis=1, keepdims=True) + eps_norm)
    unit_rows = row_block * rscale
    return (unit_rows, rscale, (unit_rows * gain_vec).astype(jnp.bfloat16))


def norm_backward(gradient, unit_rows, rscale, gain_vec):
    unit_grad = gradient * gain_vec
    back_rows = rscale * (
        unit_grad - unit_rows * jnp.mean(unit_grad * unit_rows, axis=1, keepdims=True)
    )
    return (back_rows, jnp.sum(gradient * unit_rows, axis=0))


def seq_layout(seq_lengths, row_count):
    seq_ends = jnp.cumsum(seq_lengths)
    starts = seq_ends - seq_lengths
    places = jnp.arange(row_count, dtype=jnp.int32)
    segment = jnp.sum((places[:, None] >= seq_ends[None, :]).astype(jnp.int32), axis=1)
    member = segment[:, None] == jnp.arange(seq_lengths.shape[0], dtype=jnp.int32)[None, :]
    offset = jnp.sum(jnp.where(member, starts[None, :], 0), axis=1)
    allowed = (segment[:, None] == segment[None, :]) & (places[None, :] <= places[:, None])
    return (places - offset, allowed)


def rope_tables(position, head_width):
    frequency = rope_base ** (-(jnp.arange(head_width // 2, dtype=jnp.float32) * 2.0) / head_width)
    angles = position.astype(jnp.float32)[:, None] * frequency[None, :]
    cosine = jnp.concatenate([jnp.cos(angles), jnp.cos(angles)], axis=1)[:, None, :]
    sine_table = jnp.concatenate([jnp.sin(angles), jnp.sin(angles)], axis=1)[:, None, :]
    return (cosine, sine_table)


def rotate(vectors, cosine, sine_table):
    half_width = vectors.shape[-1] // 2
    first_half = vectors[..., :half_width]
    second_half = vectors[..., half_width:]
    return vectors * cosine + jnp.concatenate([-second_half, first_half], axis=-1) * sine_table


def unrotate(gradient, cosine, sine_table):
    half_width = gradient.shape[-1] // 2
    first_half = gradient[..., :half_width]
    second_half = gradient[..., half_width:]
    return gradient * cosine + jnp.concatenate([second_half, -first_half], axis=-1) * sine_table


def score_block(query_heads, key_heads, allowed):
    row_count, head_count, head_width = query_heads.shape
    kv_count = key_heads.shape[1]
    grouped = query_heads.reshape(row_count, kv_count, head_count // kv_count, head_width)
    scores = (
        jnp.einsum("igrd,jgd->grij", grouped, key_heads, preferred_element_type=jnp.float32)
        * score_scale
    )
    return (grouped, jnp.where(allowed[None, None], scores, masked_score))


def attend(query_heads, key_heads, value_heads, allowed):
    row_count, head_count, head_width = query_heads.shape
    grouped, scores = score_block(query_heads, key_heads, allowed)
    row_max = jnp.max(scores, axis=-1, keepdims=True)
    log_total = row_max + jnp.log(jnp.sum(jnp.exp(scores - row_max), axis=-1, keepdims=True))
    prob_bf = jnp.exp(scores - log_total).astype(jnp.bfloat16)
    mixed_out = jnp.einsum(
        "grij,jgd->igrd", prob_bf, value_heads, preferred_element_type=jnp.float32
    )
    return (mixed_out.reshape(row_count, head_count * head_width).astype(jnp.bfloat16), log_total)


def attend_back(query_heads, key_heads, value_heads, allowed, log_total, mixed_grad):
    row_count, head_count, head_width = query_heads.shape
    kv_count = key_heads.shape[1]
    grouped, scores = score_block(query_heads, key_heads, allowed)
    prob_full = jnp.exp(scores - log_total)
    grad_heads = mixed_grad.reshape(row_count, kv_count, head_count // kv_count, head_width)
    dprobs = jnp.einsum(
        "igrd,jgd->grij", grad_heads, value_heads, preferred_element_type=jnp.float32
    )
    row_delta = jnp.sum(prob_full * dprobs, axis=-1, keepdims=True)
    dscores = (prob_full * (dprobs - row_delta)).astype(jnp.bfloat16)
    dquery = (
        jnp.einsum("grij,jgd->igrd", dscores, key_heads, preferred_element_type=jnp.float32)
        * score_scale
    )
    key_grad = (
        jnp.einsum("grij,igrd->jgd", dscores, grouped, preferred_element_type=jnp.float32)
        * score_scale
    )
    dvalues = jnp.einsum(
        "grij,igrd->jgd",
        prob_full.astype(jnp.bfloat16),
        grad_heads,
        preferred_element_type=jnp.float32,
    )
    return (dquery.reshape(row_count, head_count, head_width), key_grad, dvalues)


def spread_rows(row_block):
    return lax.all_gather(row_block, "tensor", axis=0, tiled=True)


def narrow(partial_rows):
    if lax.axis_size("tensor") != 2:
        return lax.psum_scatter(partial_rows, "tensor", scatter_dimension=0, tiled=True)
    half = partial_rows.shape[0] // 2
    mine = lax.axis_index("tensor")
    away = lax.dynamic_slice_in_dim(partial_rows, (1 - mine) * half, half, 0)
    kept = lax.dynamic_slice_in_dim(partial_rows, mine * half, half, 0)
    return kept + lax.ppermute(away, "tensor", [(0, 1), (1, 0)])


def split_three(values):
    high = lax.reduce_precision(values, 8, 7)
    rest = values - high
    middle = lax.reduce_precision(rest, 8, 7)
    return [part.astype(jnp.bfloat16) for part in (high, middle, rest - middle)]


def dot_f32(left, right, dims):
    return lax.dot_general(left, right, (dims, ((), ())), preferred_element_type=jnp.float32)


def exact_dot(rows_bf, values, dims):
    width = values.shape[1]
    product = dot_f32(rows_bf, jnp.concatenate(split_three(values), axis=1), dims)
    return product[:, :width] + (product[:, width : 2 * width] + product[:, 2 * width :])


def gather_dp(rows, groups):
    return lax.all_gather(rows, "dp", axis=0, tiled=True, axis_index_groups=groups)


def scatter_dp(rows, groups):
    return lax.psum_scatter(
        rows, "dp", scatter_dimension=0, tiled=True, axis_index_groups=groups
    )


def gather_weights(packed):
    return lax.all_gather(packed, "dp", axis=0, tiled=True)


def scatter_weights(packed):
    return lax.psum_scatter(packed, "dp", scatter_dimension=0, tiled=True)


def local(
    tokens,
    out_grad,
    lengths,
    routes,
    attn_gain,
    w_query,
    w_key,
    w_value,
    w_out,
    ffn_gain,
    w_router,
    w_gate,
    w_up,
    w_down,
):
    local_rows = tokens.shape[0]
    row_count = routes.shape[0]
    model_width = tokens.shape[1]
    dp_count = lax.axis_size("dp")
    replicas = max(1, dp_count // EXPERTS)
    holders = max(1, EXPERTS // dp_count)
    clusters = EXPERTS // holders
    half_ff = w_gate.shape[2]
    heads_here = w_query.shape[1] // HEAD_DIM
    kv_here = w_key.shape[1] // HEAD_DIM
    own_row = lax.axis_index("tensor") * local_rows
    groups = (
        None
        if replicas == 1
        else [[r * clusters + c for c in range(clusters)] for r in range(replicas)]
    )
    q_cols, k_cols = w_query.shape[1], w_key.shape[1]
    cuts = (q_cols, q_cols + k_cols, q_cols + 2 * k_cols)
    packed_attn = gather_weights(jnp.concatenate([w_query, w_key, w_value, w_out], axis=1))
    full_qkv = packed_attn[:, : cuts[2]]
    full_out = packed_attn[:, cuts[2] :]

    def spread_out(weight):
        grouped = weight.reshape(clusters, holders, weight.shape[1], half_ff)
        return jnp.broadcast_to(grouped[None], (replicas,) + grouped.shape).reshape(
            dp_count, holders, weight.shape[1], half_ff
        )

    def fetch(weight):
        moved = lax.all_to_all(spread_out(weight), "dp", split_axis=0, concat_axis=2, tiled=True)
        return moved.reshape(holders, model_width, half_ff)

    local_gate, local_up, local_down = fetch(w_gate), fetch(w_up), fetch(w_down)
    tokens_f32 = tokens.astype(jnp.float32)
    out_f32 = out_grad.astype(jnp.float32)
    position, allowed = seq_layout(lengths[0], row_count)
    cosine, sine_table = rope_tables(position, HEAD_DIM)
    unit_first, scale_first, normed_first = norm_forward(tokens_f32, attn_gain)
    both = spread_rows(
        jnp.concatenate(
            [normed_first, (residual_scale * out_f32).astype(jnp.bfloat16)], axis=1
        )
    )
    wide_first = both[:, :model_width]
    tagged = jnp.concatenate(
        [
            both[:, model_width:],
            jnp.pad(routes.astype(jnp.bfloat16), ((0, 0), (0, 128 - TOPK))),
        ],
        axis=1,
    )
    tagged_all = gather_dp(tagged, groups)
    moe_all = tagged_all[:, :model_width]
    routes_all = tagged_all[:, model_width : model_width + TOPK].astype(jnp.int32)
    qkv = jnp.dot(wide_first, full_qkv, preferred_element_type=jnp.float32)
    query_heads = rotate(
        qkv[:, : cuts[0]].reshape(row_count, heads_here, HEAD_DIM), cosine, sine_table
    ).astype(jnp.bfloat16)
    key_heads = rotate(
        qkv[:, cuts[0] : cuts[1]].reshape(row_count, kv_here, HEAD_DIM), cosine, sine_table
    ).astype(jnp.bfloat16)
    value_heads = qkv[:, cuts[1] :].astype(jnp.bfloat16).reshape(row_count, kv_here, HEAD_DIM)
    mixed_out, log_total = attend(query_heads, key_heads, value_heads, allowed)
    hidden = tokens_f32 + residual_scale * narrow(dot_f32(mixed_out, full_out, ((1,), (1,))))
    unit_second, scale_second, normed_second = norm_forward(hidden, ffn_gain)
    rows_all = gather_dp(spread_rows(normed_second), groups)

    expert_ids = jnp.arange(EXPERTS, dtype=jnp.int32)

    def gate_of(rows_bf, row_routes):
        picked = row_routes[:, :, None] == expert_ids[None, None, :]
        logits = exact_dot(rows_bf, w_router, ((1,), (0,)))
        named = jnp.any(picked, axis=1)
        masked = jnp.where(named, logits, -jnp.inf)
        raised = jnp.exp(masked - jnp.max(masked, axis=1, keepdims=True))
        return picked, named, raised / jnp.sum(raised, axis=1, keepdims=True)

    _, named_all, gates_all = gate_of(rows_all, routes_all)
    first_expert = lax.axis_index("dp") % clusters * holders
    out_part = back_part = gate_slots = 0.0
    grads = []
    for h in range(holders):
        gate = lax.dynamic_slice_in_dim(gates_all, first_expert + h, 1, 1)
        here = lax.dynamic_slice_in_dim(named_all, first_expert + h, 1, 1)
        gate_pre = dot_f32(rows_all, local_gate[h], ((1,), (0,)))
        up_pre = dot_f32(rows_all, local_up[h], ((1,), (0,)))
        sigmoid_gate = jax.nn.sigmoid(gate_pre)
        activated = gate_pre * sigmoid_gate
        inner_act = (activated * up_pre).astype(jnp.bfloat16)
        produced = dot_f32(inner_act, local_down[h], ((1,), (1,))).astype(jnp.bfloat16)
        produced = produced.astype(jnp.float32)
        out_part = out_part + jnp.where(here, gate * produced, 0.0)
        moe_f32 = moe_all.astype(jnp.float32)
        gate_part = jnp.sum(moe_f32 * produced, axis=1, keepdims=True)
        gate_slots = gate_slots + jnp.where(routes_all == first_expert + h, gate_part, 0.0)
        route_grad = jnp.where(here, gate * moe_f32, 0.0).astype(jnp.bfloat16)
        inner_grad = dot_f32(route_grad, local_down[h], ((1,), (0,)))
        gate_pre_grad = (
            inner_grad * up_pre * sigmoid_gate * (1.0 + gate_pre * (1.0 - sigmoid_gate))
        ).astype(jnp.bfloat16)
        up_pre_grad = (inner_grad * activated).astype(jnp.bfloat16)
        back = dot_f32(gate_pre_grad, local_gate[h], ((1,), (1,))) + dot_f32(
            up_pre_grad, local_up[h], ((1,), (1,))
        )
        back_part = back_part + back.astype(jnp.bfloat16).astype(jnp.float32)
        grads.append(
            (
                dot_f32(rows_all, gate_pre_grad, ((0,), (0,))).astype(jnp.bfloat16),
                dot_f32(rows_all, up_pre_grad, ((0,), (0,))).astype(jnp.bfloat16),
                dot_f32(route_grad, inner_act, ((0,), (0,))).astype(jnp.bfloat16),
            )
        )
    slot_parts = split_three(gate_slots)
    pad = jnp.zeros((rows_all.shape[0], 128 - 3 * TOPK), jnp.bfloat16)
    back_home = scatter_dp(
        jnp.concatenate([back_part.astype(jnp.bfloat16)] + slot_parts + [pad], axis=1), groups
    ).astype(jnp.float32)
    out_home = scatter_dp(out_part.astype(jnp.bfloat16), groups).astype(jnp.float32)
    slots = back_home[:, model_width:]
    gate_half = slots[:, :TOPK] + slots[:, TOPK : 2 * TOPK] + slots[:, 2 * TOPK : 3 * TOPK]
    own_back = narrow(
        jnp.concatenate(
            [back_home[:, :model_width], jnp.pad(gate_half, ((0, 0), (0, 128 - TOPK)))], axis=1
        )
    )
    expert_back = own_back[:, :model_width]
    gate_grad = own_back[:, model_width : model_width + TOPK]
    block_rows = (hidden + residual_scale * narrow(out_home)).astype(jnp.bfloat16)

    def send_home(index):
        stacked = jnp.stack([grads[h][index] for h in range(holders)])
        moved = lax.all_to_all(stacked[None], "dp", split_axis=2, concat_axis=0, tiled=True)
        return jnp.sum(
            moved.astype(jnp.float32).reshape(
                replicas, clusters * holders, moved.shape[2], half_ff
            ),
            axis=0,
        )

    own_routes = lax.dynamic_slice_in_dim(routes, own_row, local_rows, 0)
    picked_own, _, gates_dense = gate_of(normed_second, own_routes)
    gates_own = jnp.sum(jnp.where(picked_own, gates_dense[:, None, :], 0.0), axis=2)
    chosen_grad = gates_own * (gate_grad - jnp.sum(gates_own * gate_grad, axis=1, keepdims=True))
    logits_grad = jnp.sum(jnp.where(picked_own, chosen_grad[:, :, None], 0.0), axis=1)
    second_grad = expert_back + jnp.dot(logits_grad, w_router.T, precision=lax.Precision.HIGHEST)
    if replicas == 1:
        logits_grad_all = lax.all_gather(logits_grad, ("dp", "tensor"), axis=0, tiled=True)
        router_total = exact_dot(rows_all, logits_grad_all, ((0,), (0,)))
    else:
        router_total = lax.psum(
            exact_dot(normed_second, logits_grad, ((0,), (0,))), ("dp", "tensor")
        )
    hidden_back, ffn_gain_grad = norm_backward(second_grad, unit_second, scale_second, ffn_gain)
    hidden_grad = out_f32 + hidden_back
    attn_grad = spread_rows((residual_scale * hidden_grad).astype(jnp.bfloat16))
    mixed_grad = jnp.dot(attn_grad, full_out, preferred_element_type=jnp.float32).astype(
        jnp.bfloat16
    )
    out_w_grad = dot_f32(attn_grad, mixed_out, ((0,), (0,)))
    dquery, key_grad, dvalues = attend_back(
        query_heads, key_heads, value_heads, allowed, log_total, mixed_grad
    )
    query_grad = (
        unrotate(dquery, cosine, sine_table)
        .astype(jnp.bfloat16)
        .reshape(row_count, heads_here * HEAD_DIM)
    )
    keys_grad = (
        unrotate(key_grad, cosine, sine_table)
        .astype(jnp.bfloat16)
        .reshape(row_count, kv_here * HEAD_DIM)
    )
    value_grad = dvalues.astype(jnp.bfloat16).reshape(row_count, kv_here * HEAD_DIM)
    qkv_grad = jnp.concatenate([query_grad, keys_grad, value_grad], axis=1)
    qkv_w_grad = dot_f32(wide_first, qkv_grad, ((0,), (0,)))
    packed_grad = scatter_weights(
        jnp.concatenate([qkv_w_grad, out_w_grad], axis=1).astype(jnp.bfloat16)
    ).astype(jnp.float32)
    first_grad = narrow(dot_f32(qkv_grad, full_qkv, ((1,), (1,))))
    tokens_back, attn_gain_grad = norm_backward(first_grad, unit_first, scale_first, attn_gain)
    tokens_grad = hidden_grad + tokens_back
    attn_gain_total, ffn_gain_total = lax.psum(
        (attn_gain_grad, ffn_gain_grad), ("dp", "tensor")
    )
    return (
        block_rows,
        tokens_grad,
        attn_gain_total,
        packed_grad[:, : cuts[0]],
        packed_grad[:, cuts[0] : cuts[1]],
        packed_grad[:, cuts[1] : cuts[2]],
        packed_grad[:, cuts[2] :],
        ffn_gain_total,
        router_total,
        send_home(0),
        send_home(1),
        send_home(2),
    )


def solution(mesh):
    placed = (
        P(("dp", "tensor"), None),
        P(("dp", "tensor"), None),
        P("dp", None),
        P("dp", None),
        P(),
        P("dp", "tensor"),
        P("dp", "tensor"),
        P("dp", "tensor"),
        P("dp", "tensor"),
        P(),
        P(),
        P(None, "dp", "tensor"),
        P(None, "dp", "tensor"),
        P(None, "dp", "tensor"),
    )
    return jax.shard_map(
        local,
        mesh=mesh,
        in_specs=placed,
        out_specs=(
            P(("dp", "tensor"), None),
            P(("dp", "tensor"), None),
            P(),
            P("dp", "tensor"),
            P("dp", "tensor"),
            P("dp", "tensor"),
            P("dp", "tensor"),
            P(),
            P(),
            P(None, "dp", "tensor"),
            P(None, "dp", "tensor"),
            P(None, "dp", "tensor"),
        ),
        check_vma=False,
    )
```

time: 957 us -> 663 us (0.69)
  waiting for transfers between devices: 579 us -> 246 us
  blocking collectives: 117 us -> 219 us
  starting transfers between devices: 90.7 us -> 29.6 us
  matrix products: 48.2 us -> 66.3 us
  other arithmetic: 39.9 us -> 24.6 us
    reduce_scatter x8 -> x0, waiting for transfers between devices: 283 us -> none  [the longest x1 65.2 us: local(): lax.psum_scatter(query_w_grad, 'dp', scatter_dimension=0, tiled=True)]
    all_to_all x10 -> x4, waiting for transfers between devices: 266 us -> 72.4 us  [the longest x3 41.7 us: send_home(): lax.all_to_all(stacked[None], 'dp', split_axis=2, concat_axis=0, tiled=True)]
    unnamed x13 -> x9, waiting for transfers between devices: 2.24 us -> 120 us
    all_to_all x0 -> x2, blocking collectives: none -> 83 us  [fetch(): lax.all_to_all(spread_out(weight), 'dp', split_axis=0, concat_axis=2, til...]
    all_to_all x10 -> x4, starting transfers between devices: 89.9 us -> 23.1 us  [the longest x3 18.2 us: send_home(): lax.all_to_all(stacked[None], 'dp', split_axis=2, concat_axis=0, tiled=True)]
    all_gather x2 -> x3, waiting for transfers between devices: 0.04 us -> 34.2 us  [the longest x1 34.2 us: gather_weights(): return lax.all_gather(packed, 'dp', axis=0, tiled=True)]
    psum x1 -> x0, waiting for transfers between devices: 27.9 us -> none  [local(): lax.psum((attn_gain_grad, ffn_gain_grad, router_grad), ('dp', 'tensor'))]
    all_gather x2 -> x1, blocking collectives: 50.4 us -> 77.9 us  [local(): lax.all_gather(logits_grad, ('dp', 'tensor'), axis=0, tiled=True)]
  transfers between devices with their start and end apart: 22 -> 14, of which waited for: 15 -> 8; matrix products, arithmetic and copies ran while one was open for 12% -> 14% of each run, Pallas kernels for 0% -> 0%
where the time goes in v1:
time: 663 us; the launch traced here: 654 us
  waiting for transfers between devices  246 us (37%)
  blocking collectives  219 us (33%)
  matrix products  66.3 us (10%)
  local copies, waits for them, and re-layouts  52 us (8%)
  starting transfers between devices  29.6 us (4%)
  other arithmetic  24.6 us (4%)
  between operations  16 us (2%)
    unnamed x9, waiting for transfers between devices  120 us
    all_to_all x2, blocking collectives, fetch(): lax.all_to_all(spread_out(weight), 'dp', split_axis=0, concat_axis=2, til...  83 us
    all_gather x1, blocking collectives, local(): lax.all_gather(logits_grad, ('dp', 'tensor'), axis=0, tiled=True)  77.9 us
    dot_general x25, matrix products, dot_f32(): lax.dot_general(left, right, (dims, ((), ())), preferred_element_type=jnp...  58.6 us
    all_to_all x3, waiting for transfers between devices, send_home(): lax.all_to_all(stacked[None], 'dp', split_axis=2, concat_axis=0, tiled=True)  41.7 us
    psum x1, blocking collectives, local(): lax.psum((attn_gain_grad, ffn_gain_grad), ('dp', 'tensor'))  36.9 us
    all_gather x1, waiting for transfers between devices, gather_weights(): return lax.all_gather(packed, 'dp', axis=0, tiled=True)  34.2 us
    all_to_all x1, waiting for transfers between devices, fetch(): lax.all_to_all(spread_out(weight), 'dp', split_axis=0, concat_axis=2, til...  30.7 us
  transfers between devices with their start and end apart: 14, of which 8 were waited for; matrix products, arithmetic and copies ran while one was open for 14% of the time, Pallas kernels for 0%

profile of v1, /device:TPU:0, one launch (start us, length us, event | category | flops | bytes accessed | tf_op | source)
XLA Modules:
  0.0 654.1 jit_solution(13238016367962497329)
XLA Ops:
  7.2 1.6 pad_maximum_fusion.3
  12.6 10.0 %all_gather.21 = bf16[128,2048]{1,0:T(8,128)(2,1)S(1)} all-gather(bf16[64,2048]{1,0:T(8,128)(2,1)S(1)} %copy.200), channel_id=1, replica_groups=mesh['dp'=16,'tensor'=2] {'tensor'}, dimensions={0}, use_global_device_ids=true | all-gather | bytes 786432 | tf_op jit(solution)/shard_map/all_gather | solution.py:117
  24.8 34.2 %all-gather.5.cloned.1.call-done = bf16[1024,1536]{1,0:T(8,128)(2,1)} async-done(((bf16[64,1536]{1,0:T(8,128)(2,1)}), bf16[1024,1536]{1,0:T(8,128)(2,1)}) %all-gather.5.cloned.1.call-update) | async-done | bytes 3145744 | tf_op jit(solution)/shard_map/all_gather | solution.py:158
  59.1 2.0 fusion.24
  62.4 1.7 fusion.50
  65.1 1.5 collective-permute-start
  66.6 12.8 %collective-permute-done = f32[64,1024]{0,1:T(8,128)S(1)} collective-permute-done((f32[64,1024]{0,1:T(8,128)}, f32[64,1024]{0,1:T(8,128)S(1)}, u32[]{:S(2)}, u32[]{:S(2)}) %collective-permute-start) | collective-permute-done | bytes 262176 | tf_op jit(solution)/shard_map/ppermute | solution.py:127
  80.5 5.7 all_gather.24
  86.3 45.2 %all_to_all.72 = bf16[16,2,64,256]{3,2,1,0:T(8,128)(2,1)} all-to-all(bf16[16,2,64,256]{3,2,1,0:T(8,128)(2,1)S(1)} %bitcast.199), channel_id=1, replica_groups=mesh['dp'=16,'tensor'=2] {'dp'}, dimensions={0} | all-to-all | bytes 2097152 | tf_op jit(solution)/shard_map/all_to_all | solution.py:210
  131.5 37.7 %all_to_all.73 = bf16[16,2,64,256]{3,2,1,0:T(8,128)(2,1)S(1)} all-to-all(bf16[16,2,64,256]{3,2,1,0:T(8,128)(2,1)} %bitcast.200), channel_id=1, replica_groups=mesh['dp'=16,'tensor'=2] {'dp'}, dimensions={0} | all-to-all | bytes 2097152 | tf_op jit(solution)/shard_map/all_to_all | solution.py:210
  169.3 5.0 all-to-all-start.2
  174.3 1.6 reduce-precision_convert_fusion.3
  175.9 2.3 fusion.120
  179.3 30.7 %all-to-all-done.2 = bf16[16,2,64,256]{3,2,1,0:T(8,128)(2,1)S(1)} async-done(((bf16[16,2,64,256]{3,2,1,0:T(8,128)(2,1)}), bf16[16,2,64,256]{3,2,1,0:T(8,128)(2,1)S(1)}, u32[]{:S(2)}, u32[]{:S(2)}) %all-to-all-start.2) | async-done | bytes 1048608 | tf_op jit(solution)/shard_map/all_to_all | solution.py:210
  212.3 3.8 fusion.92
  216.3 1.3 fusion.129
  219.0 2.9 multiply_convert_fusion
  222.0 1.3 fusion.132
  223.4 1.3 fusion.127
  224.7 1.3 fusion.128
  226.1 3.3 multiply_convert_fusion.2
  229.4 1.3 fusion.131
  230.7 1.3 convolution_convert_fusion
  232.0 1.3 add_convert_fusion.1
  233.3 3.4 fusion.10
  236.7 6.8 %fusion.8 = (f32[2048]{0:T(1024)S(1)}, f32[2048]{0:T(1024)S(1)}, bf16[2048,1024]{0,1:T(8,128)(2,1)}) fusion(bf16[2048,1152]{0,1:T(8,128)(2,1)} %all-gather.7.cloned.1.call-done, bf16[2048,1024]{0,1:T(8,128)(2,1)S(1)} %convolution_convert_fusion, f32[2048]{0:T(1024)S(1)} %bitcast.223, pred[2048]{0:T(1024)(128)(4,1)S(1)} %get-tuple-element.103, ...), kind=kOutput, calls=%fused_computation.14 | convolution fusion | flops 1103097856 | bytes 14192640 | tf_op jit(solution)/shard_map/dot_general | solution.py:138
  243.5 1.4 fusion.99
  247.0 6.8 %copy.248 = bf16[2048,1152]{1,0:T(8,128)(2,1)} copy(bf16[2048,1152]{0,1:T(8,128)(2,1)} %broadcast_dynamic-update-slice_fusion) | data formatting | bytes 9437184
  253.9 6.4 copy.246
  264.2 1.3 select_reduce_fusion.1
  265.6 3.9 fusion.37
  269.8 1.3 fusion.36
  271.3 2.0 copy.223
  273.3 7.1 %all-to-all-start.3 = ((bf16[1,2,1024,256]{3,1,0,2:T(2,128)(2,1)}), bf16[1,2,1024,256]{3,1,0,2:T(2,128)(2,1)}, u32[]{:S(2)}, u32[]{:S(2)}) async-start(bf16[1,2,1024,256]{3,1,0,2:T(2,128)(2,1)} %copy.223), calls=%async_computation.3 | async-start | bytes 2097152 | tf_op jit(solution)/shard_map/all_to_all | solution.py:312
  280.4 4.4 fusion.39
  284.9 4.9 fusion.42
  289.8 2.1 fusion.45
  291.9 54.3 %reduce-scatter.12.cloned.1.call-done = bf16[128,1152]{1,0:T(8,128)(2,1)} async-done(((bf16[2048,1152]{1,0:T(8,128)(2,1)}), bf16[128,1152]{1,0:T(8,128)(2,1)}) %reduce-scatter.12.cloned.1.call-update) | async-done | bytes 294928
  348.7 1.5 collective-permute-start.2
  350.2 3.8 fusion.38
  354.2 2.0 copy.225
  356.3 65.8 %reduce-scatter.10.cloned.1.call-done = bf16[128,1024]{1,0:T(8,128)(2,1)} async-done(((bf16[2048,1024]{1,0:T(8,128)(2,1)}), bf16[128,1024]{1,0:T(8,128)(2,1)}) %reduce-scatter.10.cloned.1.call-update) | async-done | bytes 262160
  424.2 1.4 collective-permute-start.1
  427.2 2.7 multiply_reduce_fusion
  429.9 6.7 %collective-permute-done.1 = f32[64,1024]{0,1:T(8,128)} collective-permute-done((f32[64,1024]{0,1:T(8,128)}, f32[64,1024]{0,1:T(8,128)}, u32[]{:S(2)}, u32[]{:S(2)}) %collective-permute-start.1) | collective-permute-done | bytes 262176 | tf_op jit(solution)/shard_map/ppermute | solution.py:127
  436.6 2.3 multiply_convert_fusion.7
  439.1 5.6 all_gather.26
  444.7 1.5 convolution_convert_fusion.8
  447.1 4.4 all-to-all-start.4
  453.9 3.0 copy.250
  456.8 1.3 maximum_bitcast_fusion.2
  458.1 2.1 copy.227
  460.2 14.2 %all-to-all-done.4 = bf16[1,2,1024,256]{3,1,0,2:T(2,128)(2,1)} async-done(((bf16[1,2,1024,256]{3,1,0,2:T(2,128)(2,1)}), bf16[1,2,1024,256]{3,1,0,2:T(2,128)(2,1)}, u32[]{:S(2)}, u32[]{:S(2)}) %all-to-all-start.4) | async-done | bytes 1048608 | tf_op jit(solution)/shard_map/all_to_all | solution.py:312
  474.4 6.7 %all-to-all-start.5 = ((bf16[1,2,1024,256]{3,1,0,2:T(2,128)(2,1)}), bf16[1,2,1024,256]{3,1,0,2:T(2,128)(2,1)S(1)}, u32[]{:S(2)}, u32[]{:S(2)}) async-start(bf16[1,2,1024,256]{3,1,0,2:T(2,128)(2,1)} %copy.227), calls=%async_computation.5 | async-start | bytes 2097152 | tf_op jit(solution)/shard_map/all_to_all | solution.py:312
  481.1 2.1 convert_bitcast_fusion.2
  483.2 1.6 copy.224
  484.8 2.1 convert_bitcast_fusion.1
  486.9 1.6 copy.226
  488.5 27.5 %all-to-all-done.5 = bf16[1,2,1024,256]{3,1,0,2:T(2,128)(2,1)S(1)} async-done(((bf16[1,2,1024,256]{3,1,0,2:T(2,128)(2,1)}), bf16[1,2,1024,256]{3,1,0,2:T(2,128)(2,1)S(1)}, u32[]{:S(2)}, u32[]{:S(2)}) %all-to-all-start.5) | async-done | bytes 1048608 | tf_op jit(solution)/shard_map/all_to_all | solution.py:312
  517.0 1.6 copy.228
  519.5 1.6 collective-permute-start.3
  521.1 77.9 %all-gather = f32[32,64,32]{1,2,0:T(8,128)S(1)} all-gather(f32[1,64,32]{1,2,0:T(8,128)S(1)} %bitcast.212), channel_id=1, replica_groups=mesh['dp'=16,'tensor'=2] {'dp','tensor'}, dimensions={0}, use_global_device_ids=true | all-gather | bytes 270336 | tf_op jit(solution)/shard_map/all_gather | solution.py:327
  599.5 3.1 fusion.66
  605.7 36.9 %all-reduce.2 = (f32[1024]{0:T(1024)}, f32[1024]{0:T(1024)}) all-reduce(f32[1024]{0:T(1024)S(1)} %get-tuple-element.100, f32[1024]{0:T(1024)S(1)} %copy-done.46), channel_id=1, replica_groups=mesh['dp'=16,'tensor'=2] {'dp','tensor'}, use_global_device_ids=true, to_apply=%region_24.25 | all-reduce | flops 2048 | bytes 16384 | tf_op jit(solution)/shard_map/psum | solution.py:362
  (266 shorter events, 39.8 us)
Async XLA Ops:
  7.2 5.4 copy-start.47
  7.2 16.4 %copy-start.60 = (s32[1,6]{1,0:T(1,128)S(1)}, s32[1,6]{1,0:T(1,128)}, u32[]{:S(2)}) copy-start(s32[1,6]{1,0:T(1,128)} %param.16) | copy-start | bytes 76
  7.2 51.9 %all-gather.5.cloned.1.call-start = ((), (), s32[]{:S(2)}) async-start(), calls=%async_computation.9 | async-start | bytes 3342336 | tf_op jit(solution)/shard_map/all_gather | solution.py:158
  8.9 202.2 %all-gather.7.cloned.1.call-start = ((), (), s32[]{:S(2)}) async-start(), calls=%async_computation.10 | async-start | bytes 5013504 | tf_op jit(solution)/shard_map/all_gather | solution.py:148
  10.0 51.1 %copy-start.2 = (bf16[64,1024]{0,1:T(8,128)(2,1)}, bf16[64,1024]{0,1:T(8,128)(2,1)S(1)}, u32[]{:S(2)}) copy-start(bf16[64,1024]{0,1:T(8,128)(2,1)S(1)} %copy.199) | copy-start | bytes 393220
  22.6 39.1 %copy-start.6 = (bf16[128,2048]{1,0:T(8,128)(2,1)}, bf16[128,2048]{1,0:T(8,128)(2,1)S(1)}, u32[]{:S(2)}) copy-start(bf16[128,2048]{1,0:T(8,128)(2,1)S(1)} %all_gather.21) | copy-start | bytes 1572868
  23.5 188.7 %all-gather.9.cloned.1.call-start = ((), (), s32[]{:S(2)}) async-start(), calls=%async_computation.11 | async-start | bytes 4456448 | tf_op jit(solution)/shard_map/all_gather | solution.py:148
  24.7 37.6 %copy-start.22 = (f32[128,64]{0,1:T(8,128)}, f32[128,64]{0,1:T(8,128)S(1)}, u32[]{:S(2)}) copy-start(f32[128,64]{0,1:T(8,128)S(1)} %get-tuple-element.165) | copy-start | bytes 98308
  24.7 37.6 %copy-start.33 = (f32[128,64]{0,1:T(8,128)}, f32[128,64]{0,1:T(8,128)S(1)}, u32[]{:S(2)}) copy-start(f32[128,64]{0,1:T(8,128)S(1)} %get-tuple-element.153) | copy-start | bytes 98308
  61.5 18.6 %copy-start.44 = (f32[1024]{0:T(1024)S(1)}, f32[1024]{0:T(1024)}, u32[]{:S(2)}) copy-start(f32[1024]{0:T(1024)} %param.23) | copy-start | bytes 12292
  61.6 5.0 copy-start.24
  61.7 24.6 %copy-start.19 = (bf16[32,64,256]{2,1,0:T(8,128)(2,1)S(1)}, bf16[32,64,256]{2,1,0:T(8,128)(2,1)}, u32[]{:S(2)}) copy-start(bf16[32,64,256]{2,1,0:T(8,128)(2,1)} %param.25) | copy-start | bytes 3145732
  62.1 4.5 copy-start.37
  62.4 4.2 copy-start.14
  65.1 14.3 %collective-permute-start = (f32[64,1024]{0,1:T(8,128)}, f32[64,1024]{0,1:T(8,128)S(1)}, u32[]{:S(2)}, u32[]{:S(2)}) collective-permute-start(f32[64,1024]{0,1:T(8,128)} %constant_dynamic-slice_fusion.6), channel_id=1, source_target_pairs={{0,1},{1,0},{2,3},{3,2},{4,5},{5,4},{6,7},{7,6},{8,9},{9,8},{10,11... | collective-permute-start | bytes 786440 | tf_op jit(solution)/shard_map/ppermute | solution.py:127
  80.3 51.2 %copy-start.20 = (bf16[64,1024]{0,1:T(8,128)(2,1)}, bf16[64,1024]{0,1:T(8,128)(2,1)S(1)}, u32[]{:S(2)}) copy-start(bf16[64,1024]{0,1:T(8,128)(2,1)S(1)} %multiply_convert_fusion.8) | copy-start | bytes 393220
  169.3 40.8 %all-to-all-start.2 = ((bf16[16,2,64,256]{3,2,1,0:T(8,128)(2,1)}), bf16[16,2,64,256]{3,2,1,0:T(8,128)(2,1)S(1)}, u32[]{:S(2)}, u32[]{:S(2)}) async-start(bf16[16,2,64,256]{3,2,1,0:T(8,128)(2,1)} %bitcast.201), calls=%async_computation.2 | async-start | bytes 2097152 | tf_op jit(solution)/shard_map/all_to_all | solution.py:210
  174.3 172.0 %reduce-scatter.12.cloned.1.call-start = ((), (), s32[]{:S(2)}) async-start(), calls=%async_computation.13 | async-start | bytes 5013504
  212.2 24.5 %copy-start.56 = (pred[2048]{0:T(1024)(128)(4,1)}, pred[2048]{0:T(1024)(128)(4,1)S(1)}, u32[]{:S(2)}) copy-start(pred[2048]{0:T(1024)(128)(4,1)S(1)} %get-tuple-element.102) | copy-start | bytes 6148
  212.2 24.5 %copy-start.58 = (pred[2048]{0:T(1024)(128)(4,1)}, pred[2048]{0:T(1024)(128)(4,1)S(1)}, u32[]{:S(2)}) copy-start(pred[2048]{0:T(1024)(128)(4,1)S(1)} %get-tuple-element.103) | copy-start | bytes 6148
  212.3 4.1 copy-start
  212.3 4.1 copy-start.11
  216.3 20.4 %copy-start.48 = (f32[2048,1]{0,1:T(1,128)}, f32[2048,1]{0,1:T(1,128)S(1)}, u32[]{:S(2)}) copy-start(f32[2048,1]{0,1:T(1,128)S(1)} %get-tuple-element.141) | copy-start | bytes 24580
  216.3 20.4 %copy-start.50 = (f32[2048,1]{0,1:T(1,128)}, f32[2048,1]{0,1:T(1,128)S(1)}, u32[]{:S(2)}) copy-start(f32[2048,1]{0,1:T(1,128)S(1)} %get-tuple-element.142) | copy-start | bytes 24580
  222.0 10.0 %copy-start.17 = (bf16[2048,256]{1,0:T(8,128)(2,1)}, bf16[2048,256]{1,0:T(8,128)(2,1)S(1)}, u32[]{:S(2)}) copy-start(bf16[2048,256]{1,0:T(8,128)(2,1)S(1)} %get-tuple-element.122) | copy-start | bytes 3145732
  253.8 168.2 %reduce-scatter.10.cloned.1.call-start = ((), (), s32[]{:S(2)}) async-start(), calls=%async_computation.12 | async-start | bytes 4456448
  265.6 3.9 copy-start.1
  265.6 4.3 copy-start.13
  271.1 9.2 %copy-start.18 = (bf16[2048,256]{1,0:T(8,128)(2,1)S(1)}, bf16[2048,256]{1,0:T(8,128)(2,1)}, u32[]{:S(2)}) copy-start(bf16[2048,256]{1,0:T(8,128)(2,1)} %copy-done.17) | copy-start | bytes 3145732
  273.3 173.8 %all-to-all-start.3 = ((bf16[1,2,1024,256]{3,1,0,2:T(2,128)(2,1)}), bf16[1,2,1024,256]{3,1,0,2:T(2,128)(2,1)}, u32[]{:S(2)}, u32[]{:S(2)}) async-start(bf16[1,2,1024,256]{3,1,0,2:T(2,128)(2,1)} %copy.223), calls=%async_computation.3 | async-start | bytes 2097152 | tf_op jit(solution)/shard_map/all_to_all | solution.py:312
  280.4 4.5 copy-start.51
  280.4 4.5 copy-start.59
  280.4 9.4 %slice-start.2 = ((s8[4718592]{0:T(1024)(128)(4,1)}), s8[4194304]{0:T(1024)(128)(4,1)S(1)}, s32[]{:S(2)}) async-start(s8[4718592]{0:T(1024)(128)(4,1)} %bitcast.227), calls=%async_computation.17 | async-start | bytes 8388608
  284.9 4.9 copy-start.49
  284.9 4.9 copy-start.57
  284.9 4.9 slice-start.3
  284.9 4.9 copy-start.62
  348.7 5.3 copy-start.32
  348.7 76.9 %collective-permute-start.2 = (f32[64,1152]{1,0:T(8,128)}, f32[64,1152]{1,0:T(8,128)}, u32[]{:S(2)}, u32[]{:S(2)}) collective-permute-start(f32[64,1152]{1,0:T(8,128)} %copy.210), channel_id=1, source_target_pairs={{0,1},{1,0},{2,3},{3,2},{4,5},{5,4},{6,7},{7,6},{8,9},{9,8},{10,11... | collective-permute-start | bytes 884744 | tf_op jit(solution)/shard_map/ppermute | solution.py:127
  354.0 73.0 %copy-start.43 = (f32[64,8]{0,1:T(8,128)S(1)}, f32[64,8]{0,1:T(8,128)}, u32[]{:S(2)}) copy-start(f32[64,8]{0,1:T(8,128)} %select_reduce_fusion.1) | copy-start | bytes 6148
  354.1 73.1 %copy-start.41 = (s32[64,8]{0,1:T(8,128)S(1)}, s32[64,8]{0,1:T(8,128)}, u32[]{:S(2)}) copy-start(s32[64,8]{0,1:T(8,128)} %copy-done.40) | copy-start | bytes 6148
  354.1 73.1 %copy-start.45 = (f32[1024]{0:T(1024)S(1)}, f32[1024]{0:T(1024)}, u32[]{:S(2)}) copy-start(f32[1024]{0:T(1024)} %param.23) | copy-start | bytes 12292
  354.1 73.1 %copy-start.55 = (f32[64]{0:T(128)S(1)}, f32[64]{0:T(128)}, u32[]{:S(2)}) copy-start(f32[64]{0:T(128)} %copy-done.54) | copy-start | bytes 772
  354.2 82.4 %copy-start.3 = (bf16[64,1024]{0,1:T(8,128)(2,1)S(1)}, bf16[64,1024]{0,1:T(8,128)(2,1)}, u32[]{:S(2)}) copy-start(bf16[64,1024]{0,1:T(8,128)(2,1)} %copy-done.2) | copy-start | bytes 393220
  424.2 12.4 %collective-permute-start.1 = (f32[64,1024]{0,1:T(8,128)}, f32[64,1024]{0,1:T(8,128)}, u32[]{:S(2)}, u32[]{:S(2)}) collective-permute-start(f32[64,1024]{0,1:T(8,128)} %constant_dynamic-slice_fusion.3), channel_id=1, source_target_pairs={{0,1},{1,0},{2,3},{3,2},{4,5},{5,4},{6,7},{7,6},{8,9},{9,8},{10,11... | collective-permute-start | bytes 786440 | tf_op jit(solution)/shard_map/ppermute | solution.py:127
  427.1 19.3 %copy-start.27 = (bf16[128,256]{0,1:T(8,128)(2,1)S(1)}, bf16[128,256]{0,1:T(8,128)(2,1)}, u32[]{:S(2)}) copy-start(bf16[128,256]{0,1:T(8,128)(2,1)} %copy-done.26) | copy-start | bytes 196612
  427.1 19.3 %copy-start.38 = (f32[1,8,128]{2,1,0:T(8,128)S(1)}, f32[1,8,128]{2,1,0:T(8,128)}, u32[]{:S(2)}) copy-start(f32[1,8,128]{2,1,0:T(8,128)} %copy-done.37) | copy-start | bytes 12292
  436.6 10.2 %copy-start.25 = (bf16[128,4,64,1]{0,2,3,1:T(8,128)(2,1)S(1)}, bf16[128,4,64,1]{0,2,3,1:T(8,128)(2,1)}, u32[]{:S(2)}) copy-start(bf16[128,4,64,1]{0,2,3,1:T(8,128)(2,1)} %copy-done.24) | copy-start | bytes 196612
  439.0 12.8 %copy-start.23 = (f32[128,64]{0,1:T(8,128)S(1)}, f32[128,64]{0,1:T(8,128)}, u32[]{:S(2)}) copy-start(f32[128,64]{0,1:T(8,128)} %copy-done.22) | copy-start | bytes 98308
  444.7 7.1 %copy-start.34 = (f32[128,64]{0,1:T(8,128)S(1)}, f32[128,64]{0,1:T(8,128)}, u32[]{:S(2)}) copy-start(f32[128,64]{0,1:T(8,128)} %copy-done.33) | copy-start | bytes 98308
  446.3 5.8 copy-start.36
  446.4 5.7 copy-start.39
  446.7 5.7 copy-start.15
  446.9 6.0 copy-start.7
  447.1 27.3 %all-to-all-start.4 = ((bf16[1,2,1024,256]{3,1,0,2:T(2,128)(2,1)}), bf16[1,2,1024,256]{3,1,0,2:T(2,128)(2,1)}, u32[]{:S(2)}, u32[]{:S(2)}) async-start(bf16[1,2,1024,256]{3,1,0,2:T(2,128)(2,1)} %copy.225), calls=%async_computation.4 | async-start | bytes 2097152 | tf_op jit(solution)/shard_map/all_to_all | solution.py:312
  451.5 191.1 %reduce-scatter.14.cloned.1.call-start = ((), (), s32[]{:S(2)}) async-start(), calls=%async_computation.14 | async-start | bytes 3342336
  474.4 41.7 %all-to-all-start.5 = ((bf16[1,2,1024,256]{3,1,0,2:T(2,128)(2,1)}), bf16[1,2,1024,256]{3,1,0,2:T(2,128)(2,1)S(1)}, u32[]{:S(2)}, u32[]{:S(2)}) async-start(bf16[1,2,1024,256]{3,1,0,2:T(2,128)(2,1)} %copy.227), calls=%async_computation.5 | async-start | bytes 2097152 | tf_op jit(solution)/shard_map/all_to_all | solution.py:312
  488.5 30.0 %copy-start.29 = (bf16[128,512]{0,1:T(8,128)(2,1)S(1)}, bf16[128,512]{0,1:T(8,128)(2,1)}, u32[]{:S(2)}) copy-start(bf16[128,512]{0,1:T(8,128)(2,1)} %copy-done.28) | copy-start | bytes 393220
  519.5 83.1 %copy-start.21 = (bf16[64,1024]{0,1:T(8,128)(2,1)S(1)}, bf16[64,1024]{0,1:T(8,128)(2,1)}, u32[]{:S(2)}) copy-start(bf16[64,1024]{0,1:T(8,128)(2,1)} %get-tuple-element.131) | copy-start | bytes 393220
  519.5 84.6 %collective-permute-start.3 = (f32[64,1024]{0,1:T(8,128)S(1)}, f32[64,1024]{0,1:T(8,128)S(1)}, u32[]{:S(2)}, u32[]{:S(2)}) collective-permute-start(f32[64,1024]{0,1:T(8,128)S(1)} %constant_dynamic-slice_fusion), channel_id=1, source_target_pairs={{0,1},{1,0},{2,3},{3,2},{4,5},{5,4},{6,7},{7,6},{8,9},{9,8},{10,11... | collective-permute-start | bytes 786440 | tf_op jit(solution)/shard_map/ppermute | solution.py:127
  599.0 5.1 copy-start.42
  599.0 5.1 copy-start.53
  599.5 5.1 copy-start.5
  599.5 6.2 copy-start.46
  (17 other events, 31.1 us)
Sparse Core Ops, SparseCore 0:
  10.9 48.1 all-gather.4
  61.2 71.3 all-gather.6
  134.8 75.2 all-gather.8
  253.9 92.2 reduce-scatter.11
  349.9 72.0 reduce-scatter.9
  457.0 79.1 reduce-scatter.13

commit v2 on v1

--- a/solution.py
+++ b/solution.py
@@ -1,6 +1,8 @@
 import jax
 import jax.numpy as jnp
 from jax import lax
+from jax.experimental import pallas as pl
+from jax.experimental.pallas import tpu as pltpu
 from jax.sharding import PartitionSpec as P
 
 EXPERTS = 32
@@ -160,6 +162,67 @@
 
 def scatter_weights(packed):
     return lax.psum_scatter(packed, "dp", scatter_dimension=0, tiled=True)
+
+
+def share_kernel(x_ref, o_ref, send_sem, recv_sem, own_sem):
+    width = lax.axis_size("tensor")
+    count = lax.axis_size("dp") * width
+    me = lax.axis_index("dp") * width + lax.axis_index("tensor")
+    barrier = pltpu.get_barrier_semaphore()
+
+    def place(k):
+        peer = lax.rem(me + k, count)
+        return (lax.div(peer, width), lax.rem(peer, width))
+
+    def greet(k, carry):
+        pl.semaphore_signal(
+            barrier, inc=1, device_id=place(k), device_id_type=pl.DeviceIdType.MESH
+        )
+        return carry
+
+    def copy(k, slot):
+        return pltpu.make_async_remote_copy(
+            src_ref=x_ref,
+            dst_ref=o_ref.at[slot],
+            send_sem=send_sem.at[k],
+            recv_sem=recv_sem.at[k],
+            device_id=place(k),
+            device_id_type=pl.DeviceIdType.MESH,
+        )
+
+    def start(k, carry):
+        copy(k, me).start()
+        return carry
+
+    def finish(k, carry):
+        copy(k, me).wait_send()
+        copy(k, lax.rem(me - k + count, count)).wait_recv()
+        return carry
+
+    lax.fori_loop(1, count, greet, 0)
+    pl.semaphore_wait(barrier, count - 1)
+    own = pltpu.make_async_copy(x_ref, o_ref.at[me], own_sem)
+    own.start()
+    lax.fori_loop(1, count, start, 0)
+    lax.fori_loop(1, count, finish, 0)
+    own.wait()
+
+
+def share(block):
+    count = lax.axis_size("dp") * lax.axis_size("tensor")
+    return pl.pallas_call(
+        share_kernel,
+        out_shape=jax.ShapeDtypeStruct((count,) + block.shape, block.dtype),
+        in_specs=[pl.BlockSpec(memory_space=pltpu.VMEM)],
+        out_specs=pl.BlockSpec(memory_space=pltpu.VMEM),
+        scratch_shapes=[
+            pltpu.SemaphoreType.DMA((count,)),
+            pltpu.SemaphoreType.DMA((count,)),
+            pltpu.SemaphoreType.DMA,
+        ],
+        compiler_params=pltpu.CompilerParams(collective_id=0, has_side_effects=True),
+        name="share",
+    )(block)
 
 
 def local(
@@ -292,10 +355,15 @@
         )
     slot_parts = split_three(gate_slots)
     pad = jnp.zeros((rows_all.shape[0], 128 - 3 * TOPK), jnp.bfloat16)
-    back_home = scatter_dp(
-        jnp.concatenate([back_part.astype(jnp.bfloat16)] + slot_parts + [pad], axis=1), groups
+    home = scatter_dp(
+        jnp.concatenate(
+            [back_part.astype(jnp.bfloat16)] + slot_parts + [pad, out_part.astype(jnp.bfloat16)],
+            axis=1,
+        ),
+        groups,
     ).astype(jnp.float32)
-    out_home = scatter_dp(out_part.astype(jnp.bfloat16), groups).astype(jnp.float32)
+    back_home = home[:, : model_width + 128]
+    out_home = home[:, model_width + 128 :]
     slots = back_home[:, model_width:]
     gate_half = slots[:, :TOPK] + slots[:, TOPK : 2 * TOPK] + slots[:, 2 * TOPK : 3 * TOPK]
     own_back = narrow(
@@ -323,13 +391,6 @@
     chosen_grad = gates_own * (gate_grad - jnp.sum(gates_own * gate_grad, axis=1, keepdims=True))
     logits_grad = jnp.sum(jnp.where(picked_own, chosen_grad[:, :, None], 0.0), axis=1)
     second_grad = expert_back + jnp.dot(logits_grad, w_router.T, precision=lax.Precision.HIGHEST)
-    if replicas == 1:
-        logits_grad_all = lax.all_gather(logits_grad, ("dp", "tensor"), axis=0, tiled=True)
-        router_total = exact_dot(rows_all, logits_grad_all, ((0,), (0,)))
-    else:
-        router_total = lax.psum(
-            exact_dot(normed_second, logits_grad, ((0,), (0,))), ("dp", "tensor")
-        )
     hidden_back, ffn_gain_grad = norm_backward(second_grad, unit_second, scale_second, ffn_gain)
     hidden_grad = out_f32 + hidden_back
     attn_grad = spread_rows((residual_scale * hidden_grad).astype(jnp.bfloat16))
@@ -359,9 +420,32 @@
     first_grad = narrow(dot_f32(qkv_grad, full_qkv, ((1,), (1,))))
     tokens_back, attn_gain_grad = norm_backward(first_grad, unit_first, scale_first, attn_gain)
     tokens_grad = hidden_grad + tokens_back
-    attn_gain_total, ffn_gain_total = lax.psum(
-        (attn_gain_grad, ffn_gain_grad), ("dp", "tensor")
-    )
+    if replicas == 1:
+        tall = local_rows * EXPERTS // 128
+        wide = model_width // 128
+        shared = share(
+            jnp.concatenate(
+                [
+                    logits_grad.reshape(tall, 128),
+                    attn_gain_grad.reshape(wide, 128),
+                    ffn_gain_grad.reshape(wide, 128),
+                ],
+                axis=0,
+            )
+        )
+        logits_grad_all = shared[:, :tall].reshape(rows_all.shape[0], EXPERTS)
+        router_total = exact_dot(rows_all, logits_grad_all, ((0,), (0,)))
+        gains = jnp.sum(shared[:, tall:], axis=0).reshape(2, model_width)
+        attn_gain_total, ffn_gain_total = gains[0], gains[1]
+    else:
+        attn_gain_total, ffn_gain_total, router_total = lax.psum(
+            (
+                attn_gain_grad,
+                ffn_gain_grad,
+                exact_dot(normed_second, logits_grad, ((0,), (0,))),
+            ),
+            ("dp", "tensor"),
+        )
     return (
         block_rows,
         tokens_grad,

time: 663 us -> 535 us (0.81)
  blocking collectives: 219 us -> 104 us
  waiting for transfers between devices: 246 us -> 213 us
  Pallas kernels: 0 us -> 18.2 us
    all_gather x1 -> x0, blocking collectives: 77.9 us -> none  [local(): lax.all_gather(logits_grad, ('dp', 'tensor'), axis=0, tiled=True)]
    psum x1 -> x0, blocking collectives: 36.9 us -> none  [local(): lax.psum((attn_gain_grad, ffn_gain_grad), ('dp', 'tensor'))]
    unnamed x9 -> x7, waiting for transfers between devices: 120 us -> 89.6 us
    pallas_call x0 -> x1, Pallas kernels: none -> 18.2 us  [share(): pl.pallas_call(share_kernel, out_shape=jax.ShapeDtypeStruct((count,) + bl...]
    unnamed x150 -> x144, local copies, waits for them, and re-layouts: 28.8 us -> 27.6 us
  transfers between devices with their start and end apart: 14 -> 13, of which waited for: 8 -> 7; matrix products, arithmetic and copies ran while one was open for 14% -> 18% of each run, Pallas kernels for 0% -> 3%
where the time goes in v2:
time: 535 us; the launch traced here: 527 us
  waiting for transfers between devices  213 us (40%)
  blocking collectives  104 us (19%)
  matrix products  62.5 us (12%)
  local copies, waits for them, and re-layouts  53.4 us (10%)
  other arithmetic  30.7 us (6%)
  starting transfers between devices  28.6 us (5%)
  Pallas kernels  18.2 us (3%)
  between operations  15.7 us (3%)
    unnamed x7, waiting for transfers between devices  89.6 us
    all_to_all x2, blocking collectives, fetch(): lax.all_to_all(spread_out(weight), 'dp', split_axis=0, concat_axis=2, til...  83 us
    dot_general x25, matrix products, dot_f32(): lax.dot_general(left, right, (dims, ((), ())), preferred_element_type=jnp...  54 us
    all_to_all x3, waiting for transfers between devices, send_home(): lax.all_to_all(stacked[None], 'dp', split_axis=2, concat_axis=0, tiled=True)  39.9 us
    all_gather x1, waiting for transfers between devices, gather_weights(): return lax.all_gather(packed, 'dp', axis=0, tiled=True)  34.3 us
    all_to_all x1, waiting for transfers between devices, fetch(): lax.all_to_all(spread_out(weight), 'dp', split_axis=0, concat_axis=2, til...  29.8 us
    unnamed x144, local copies, waits for them, and re-layouts  27.6 us
    all_gather x3, blocking collectives, spread_rows(): return lax.all_gather(row_block, 'tensor', axis=0, tiled=True)  21.3 us
  transfers between devices with their start and end apart: 13, of which 7 were waited for; matrix products, arithmetic and copies ran while one was open for 18% of the time, Pallas kernels for 3%

profile of v2, /device:TPU:0, one launch (start us, length us, event | category | flops | bytes accessed | tf_op | source)
XLA Modules:
  0.0 526.6 jit_solution(397238035099600605)
XLA Ops:
  7.2 1.6 pad_maximum_fusion.3
  12.5 10.0 %all_gather.18 = bf16[128,2048]{1,0:T(8,128)(2,1)S(1)} all-gather(bf16[64,2048]{1,0:T(8,128)(2,1)S(1)} %copy.174), channel_id=1, replica_groups=mesh['dp'=16,'tensor'=2] {'tensor'}, dimensions={0}, use_global_device_ids=true | all-gather | bytes 786432 | tf_op jit(solution)/shard_map/all_gather | solution.py:119
  24.7 34.3 %all-gather.4.cloned.1.call-done = bf16[1024,1536]{1,0:T(8,128)(2,1)} async-done(((bf16[64,1536]{1,0:T(8,128)(2,1)}), bf16[1024,1536]{1,0:T(8,128)(2,1)}) %all-gather.4.cloned.1.call-update) | async-done | bytes 3145744 | tf_op jit(solution)/shard_map/all_gather | solution.py:160
  59.1 2.0 fusion.25
  62.7 1.7 fusion.51
  64.6 1.5 collective-permute-start
  66.1 12.7 %collective-permute-done = f32[64,1024]{0,1:T(8,128)} collective-permute-done((f32[64,1024]{0,1:T(8,128)S(1)}, f32[64,1024]{0,1:T(8,128)}, u32[]{:S(2)}, u32[]{:S(2)}) %collective-permute-start) | collective-permute-done | bytes 262176 | tf_op jit(solution)/shard_map/ppermute | solution.py:129
  80.5 5.7 %all_gather.21 = bf16[128,1024]{1,0:T(8,128)(2,1)} all-gather(bf16[64,1024]{1,0:T(8,128)(2,1)S(1)} %copy.183), channel_id=1, replica_groups=mesh['dp'=16,'tensor'=2] {'tensor'}, dimensions={0}, use_global_device_ids=true | all-gather | bytes 393216 | tf_op jit(solution)/shard_map/all_gather | solution.py:119
  86.3 45.2 %all_to_all.72 = bf16[16,2,64,256]{3,2,1,0:T(8,128)(2,1)} all-to-all(bf16[16,2,64,256]{3,2,1,0:T(8,128)(2,1)S(1)} %bitcast.201), channel_id=1, replica_groups=mesh['dp'=16,'tensor'=2] {'dp'}, dimensions={0} | all-to-all | bytes 2097152 | tf_op jit(solution)/shard_map/all_to_all | solution.py:273
  131.4 37.9 %all_to_all.73 = bf16[16,2,64,256]{3,2,1,0:T(8,128)(2,1)} all-to-all(bf16[16,2,64,256]{3,2,1,0:T(8,128)(2,1)} %bitcast.202), channel_id=1, replica_groups=mesh['dp'=16,'tensor'=2] {'dp'}, dimensions={0} | all-to-all | bytes 2097152 | tf_op jit(solution)/shard_map/all_to_all | solution.py:273
  169.3 5.0 all-to-all-start.1
  175.5 2.3 fusion.122
  177.9 2.3 fusion.121
  180.1 29.8 %all-to-all-done.1 = bf16[16,2,64,256]{3,2,1,0:T(8,128)(2,1)S(1)} async-done(((bf16[16,2,64,256]{3,2,1,0:T(8,128)(2,1)}), bf16[16,2,64,256]{3,2,1,0:T(8,128)(2,1)S(1)}, u32[]{:S(2)}, u32[]{:S(2)}) %all-to-all-start.1) | async-done | bytes 1048608 | tf_op jit(solution)/shard_map/all_to_all | solution.py:273
  212.2 3.7 fusion.93
  216.2 1.3 fusion.132
  218.5 1.5 fusion.14
  220.0 2.2 multiply_convert_fusion
  222.2 1.3 fusion.133
  223.6 1.3 fusion.130
  225.0 1.5 fusion.18
  226.5 2.4 multiply_convert_fusion.1
  228.8 1.3 fusion.131
  230.2 1.3 convolution_convert_fusion
  231.5 1.4 add_convert_fusion.1
  232.9 3.4 fusion.10
  236.3 3.9 fusion.8
  240.1 1.4 fusion.100
  243.6 3.7 fusion.11
  247.3 11.7 %copy.222 = bf16[2048,2176]{1,0:T(8,128)(2,1)} copy(bf16[2048,2176]{0,1:T(8,128)(2,1)} %fusion.11) | data formatting | bytes 17825792
  260.9 3.6 fusion.38
  264.6 1.3 fusion.37
  266.0 2.0 copy.199
  268.1 7.0 %all-to-all-start.3 = ((bf16[1,2,1024,256]{3,1,0,2:T(2,128)(2,1)}), bf16[1,2,1024,256]{3,1,0,2:T(2,128)(2,1)}, u32[]{:S(2)}, u32[]{:S(2)}) async-start(bf16[1,2,1024,256]{3,1,0,2:T(2,128)(2,1)} %copy.199), calls=%async_computation.3 | async-start | bytes 2097152 | tf_op jit(solution)/shard_map/all_to_all | solution.py:380
  275.1 5.3 %fusion.40 = bf16[1,1024,256]{2,1,0:T(8,128)(2,1)} fusion(bf16[2048,1024]{1,0:T(8,128)(2,1)} %all-gather.8.cloned.1.call-done, bf16[2048,256]{1,0:T(8,128)(2,1)} %copy-done.17), kind=kOutput, calls=%fused_computation.62 | convolution fusion | flops 1074003968 | bytes 5767168 | tf_op jit(solution)/shard_map/dot_general | solution.py:140
  280.4 4.8 fusion.43
  285.3 2.1 fusion.46
  287.3 89.6 %reduce-scatter.7.cloned.1.call-done = bf16[128,2176]{1,0:T(8,128)(2,1)} async-done(((bf16[2048,2176]{1,0:T(8,128)(2,1)}), bf16[128,2176]{1,0:T(8,128)(2,1)}) %reduce-scatter.7.cloned.1.call-update) | async-done | bytes 557072
  376.9 1.4 copy.223
  379.5 2.0 copy.184
  381.5 1.5 collective-permute-start.2
  383.0 3.8 fusion.39
  386.9 2.0 copy.201
  390.5 2.0 copy.185
  393.9 2.7 multiply_reduce_fusion
  396.7 6.7 %collective-permute-done.1 = f32[64,1024]{0,1:T(8,128)} collective-permute-done((f32[64,1024]{0,1:T(8,128)}, f32[64,1024]{0,1:T(8,128)}, u32[]{:S(2)}, u32[]{:S(2)}) %collective-permute-start.1) | collective-permute-done | bytes 262176 | tf_op jit(solution)/shard_map/ppermute | solution.py:129
  403.4 2.3 multiply_convert_fusion.7
  405.8 5.6 %all_gather.23 = bf16[128,1024]{1,0:T(8,128)(2,1)S(1)} all-gather(bf16[64,1024]{1,0:T(8,128)(2,1)S(1)} %copy.189), channel_id=1, replica_groups=mesh['dp'=16,'tensor'=2] {'tensor'}, dimensions={0}, use_global_device_ids=true | all-gather | bytes 393216 | tf_op jit(solution)/shard_map/all_gather | solution.py:119
  411.4 1.5 convolution_convert_fusion.8
  414.6 4.9 all-to-all-start.4
  422.1 3.0 copy.224
  425.1 1.3 maximum_bitcast_fusion.2
  426.4 2.0 copy.203
  428.5 14.0 %all-to-all-done.4 = bf16[1,2,1024,256]{3,1,0,2:T(2,128)(2,1)} async-done(((bf16[1,2,1024,256]{3,1,0,2:T(2,128)(2,1)}), bf16[1,2,1024,256]{3,1,0,2:T(2,128)(2,1)}, u32[]{:S(2)}, u32[]{:S(2)}) %all-to-all-start.4) | async-done | bytes 1048608 | tf_op jit(solution)/shard_map/all_to_all | solution.py:380
  442.5 6.8 %all-to-all-start.5 = ((bf16[1,2,1024,256]{3,1,0,2:T(2,128)(2,1)}), bf16[1,2,1024,256]{3,1,0,2:T(2,128)(2,1)S(1)}, u32[]{:S(2)}, u32[]{:S(2)}) async-start(bf16[1,2,1024,256]{3,1,0,2:T(2,128)(2,1)} %copy.203), calls=%async_computation.5 | async-start | bytes 2097152 | tf_op jit(solution)/shard_map/all_to_all | solution.py:380
  449.3 2.1 convert_bitcast_fusion.2
  451.4 1.6 copy.200
  453.0 2.5 convert_bitcast_fusion.1
  455.5 1.6 copy.202
  458.5 25.9 %all-to-all-done.5 = bf16[1,2,1024,256]{3,1,0,2:T(2,128)(2,1)S(1)} async-done(((bf16[1,2,1024,256]{3,1,0,2:T(2,128)(2,1)}), bf16[1,2,1024,256]{3,1,0,2:T(2,128)(2,1)S(1)}, u32[]{:S(2)}, u32[]{:S(2)}) %all-to-all-start.5) | async-done | bytes 1048608 | tf_op jit(solution)/shard_map/all_to_all | solution.py:380
  485.3 1.6 copy.204
  487.9 1.6 fusion.64
  491.2 18.2 %share.1 = f32[32,32,128]{2,1,0:T(8,128)} custom-call(f32[32,128]{1,0:T(8,128)} %pad_maximum_fusion.11.x_ref), custom_call_target="tpu_custom_call" | custom-call | tf_op jit(solution)/shard_map/share/pallas_call | solution.py:213
  511.8 3.0 fusion.67
  (261 shorter events, 38.3 us)
Async XLA Ops:
  7.2 5.3 %copy-start.53 = (s32[128,8]{0,1:T(8,128)S(1)}, s32[128,8]{0,1:T(8,128)}, u32[]{:S(2)}) copy-start(s32[128,8]{0,1:T(8,128)} %param.17) | copy-start | bytes 12292
  7.2 16.3 %copy-start.58 = (s32[1,6]{1,0:T(1,128)S(1)}, s32[1,6]{1,0:T(1,128)}, u32[]{:S(2)}) copy-start(s32[1,6]{1,0:T(1,128)} %param.16) | copy-start | bytes 76
  7.2 51.9 %all-gather.4.cloned.1.call-start = ((), (), s32[]{:S(2)}) async-start(), calls=%async_computation.8 | async-start | bytes 3342336 | tf_op jit(solution)/shard_map/all_gather | solution.py:160
  8.9 202.1 %all-gather.6.cloned.1.call-start = ((), (), s32[]{:S(2)}) async-start(), calls=%async_computation.9 | async-start | bytes 5013504 | tf_op jit(solution)/shard_map/all_gather | solution.py:150
  22.5 38.8 %copy-start.6 = (bf16[128,2048]{1,0:T(8,128)(2,1)}, bf16[128,2048]{1,0:T(8,128)(2,1)S(1)}, u32[]{:S(2)}) copy-start(bf16[128,2048]{1,0:T(8,128)(2,1)S(1)} %all_gather.18) | copy-start | bytes 1572868
  23.4 188.7 %all-gather.8.cloned.1.call-start = ((), (), s32[]{:S(2)}) async-start(), calls=%async_computation.10 | async-start | bytes 4456448 | tf_op jit(solution)/shard_map/all_gather | solution.py:150
  24.6 37.7 %copy-start.30 = (f32[128,64]{0,1:T(8,128)}, f32[128,64]{0,1:T(8,128)S(1)}, u32[]{:S(2)}) copy-start(f32[128,64]{0,1:T(8,128)S(1)} %get-tuple-element.142) | copy-start | bytes 98308
  61.6 18.5 %copy-start.50 = (f32[1024]{0:T(1024)S(1)}, f32[1024]{0:T(1024)}, u32[]{:S(2)}) copy-start(f32[1024]{0:T(1024)} %param.23) | copy-start | bytes 12292
  61.6 18.7 %copy-start.22 = (bf16[128,4,64,1]{0,2,3,1:T(8,128)(2,1)}, bf16[128,4,64,1]{0,2,3,1:T(8,128)(2,1)S(1)}, u32[]{:S(2)}) copy-start(bf16[128,4,64,1]{0,2,3,1:T(8,128)(2,1)S(1)} %fusion.97) | copy-start | bytes 196612
  61.7 24.5 %copy-start.18 = (bf16[32,64,256]{2,1,0:T(8,128)(2,1)S(1)}, bf16[32,64,256]{2,1,0:T(8,128)(2,1)}, u32[]{:S(2)}) copy-start(bf16[32,64,256]{2,1,0:T(8,128)(2,1)} %param.25) | copy-start | bytes 3145732
  64.6 14.2 %collective-permute-start = (f32[64,1024]{0,1:T(8,128)S(1)}, f32[64,1024]{0,1:T(8,128)}, u32[]{:S(2)}, u32[]{:S(2)}) collective-permute-start(f32[64,1024]{0,1:T(8,128)S(1)} %constant_dynamic-slice_fusion.6), channel_id=1, source_target_pairs={{0,1},{1,0},{2,3},{3,2},{4,5},{5,4},{6,7},{7,6},{8,9},{9,8},{10,11... | collective-permute-start | bytes 786440 | tf_op jit(solution)/shard_map/ppermute | solution.py:129
  80.1 94.7 %copy-start.25 = (f32[1024,32]{0,1:T(8,128)S(1)}, f32[1024,32]{0,1:T(8,128)}, u32[]{:S(2)}) copy-start(f32[1024,32]{0,1:T(8,128)} %param.24) | copy-start | bytes 393220
  80.1 95.4 %copy-start.56 = (f32[64]{0:T(128)}, f32[64]{0:T(128)S(1)}, u32[]{:S(2)}) copy-start(f32[64]{0:T(128)S(1)} %add_rsqrt_fusion) | copy-start | bytes 772
  80.3 97.5 %copy-start.19 = (bf16[64,1024]{0,1:T(8,128)(2,1)}, bf16[64,1024]{0,1:T(8,128)(2,1)S(1)}, u32[]{:S(2)}) copy-start(bf16[64,1024]{0,1:T(8,128)(2,1)S(1)} %multiply_convert_fusion.8) | copy-start | bytes 393220
  169.3 40.6 %all-to-all-start.1 = ((bf16[16,2,64,256]{3,2,1,0:T(8,128)(2,1)}), bf16[16,2,64,256]{3,2,1,0:T(8,128)(2,1)S(1)}, u32[]{:S(2)}, u32[]{:S(2)}) async-start(bf16[16,2,64,256]{3,2,1,0:T(8,128)(2,1)} %bitcast.203), calls=%async_computation.1 | async-start | bytes 2097152 | tf_op jit(solution)/shard_map/all_to_all | solution.py:273
  174.3 202.6 %reduce-scatter.7.cloned.1.call-start = ((), (), s32[]{:S(2)}) async-start(), calls=%async_computation.11 | async-start | bytes 9469952
  175.5 40.4 %copy-start.33 = (bf16[1024,32]{0,1:T(8,128)(2,1)}, bf16[1024,32]{0,1:T(8,128)(2,1)S(1)}, u32[]{:S(2)}) copy-start(bf16[1024,32]{0,1:T(8,128)(2,1)S(1)} %get-tuple-element.136) | copy-start | bytes 196612
  175.5 40.4 %copy-start.35 = (bf16[1024,32]{0,1:T(8,128)(2,1)}, bf16[1024,32]{0,1:T(8,128)(2,1)S(1)}, u32[]{:S(2)}) copy-start(bf16[1024,32]{0,1:T(8,128)(2,1)S(1)} %get-tuple-element.137) | copy-start | bytes 196612
  175.5 36.6 %copy-start.37 = (bf16[1024,32]{0,1:T(8,128)(2,1)S(1)}, bf16[1024,32]{0,1:T(8,128)(2,1)}, u32[]{:S(2)}) copy-start(bf16[1024,32]{0,1:T(8,128)(2,1)} %get-tuple-element.138) | copy-start | bytes 196612
  212.1 4.1 copy-start
  212.2 4.1 copy-start.11
  215.9 2.2 slice-start
  216.1 2.2 copy-start.9
  216.2 2.2 slice-start.1
  218.5 1.5 copy-start.4
  222.2 8.0 %copy-start.2 = (bf16[2048,256]{1,0:T(8,128)(2,1)}, bf16[2048,256]{1,0:T(8,128)(2,1)S(1)}, u32[]{:S(2)}) copy-start(bf16[2048,256]{1,0:T(8,128)(2,1)S(1)} %get-tuple-element.104) | copy-start | bytes 3145732
  222.2 9.3 %copy-start.17 = (bf16[2048,256]{1,0:T(8,128)(2,1)}, bf16[2048,256]{1,0:T(8,128)(2,1)S(1)}, u32[]{:S(2)}) copy-start(bf16[2048,256]{1,0:T(8,128)(2,1)S(1)} %get-tuple-element.106) | copy-start | bytes 3145732
  224.9 1.5 copy-start.10
  228.8 4.0 copy-start.16
  228.8 7.4 %copy-start.59 = (bf16[2048,256]{1,0:T(8,128)(2,1)}, bf16[2048,256]{1,0:T(8,128)(2,1)S(1)}, u32[]{:S(2)}) copy-start(bf16[2048,256]{1,0:T(8,128)(2,1)S(1)} %get-tuple-element.107) | copy-start | bytes 3145732
  259.0 1.8 copy-start.13
  259.2 1.6 copy-start.47
  260.8 3.7 copy-start.1
  260.9 3.7 copy-start.15
  268.1 146.6 %all-to-all-start.3 = ((bf16[1,2,1024,256]{3,1,0,2:T(2,128)(2,1)}), bf16[1,2,1024,256]{3,1,0,2:T(2,128)(2,1)}, u32[]{:S(2)}, u32[]{:S(2)}) async-start(bf16[1,2,1024,256]{3,1,0,2:T(2,128)(2,1)} %copy.199), calls=%async_computation.3 | async-start | bytes 2097152 | tf_op jit(solution)/shard_map/all_to_all | solution.py:380
  275.1 5.3 %copy-start.3 = (bf16[2048,256]{1,0:T(8,128)(2,1)S(1)}, bf16[2048,256]{1,0:T(8,128)(2,1)}, u32[]{:S(2)}) copy-start(bf16[2048,256]{1,0:T(8,128)(2,1)} %copy-done.2) | copy-start | bytes 3145732
  275.1 10.1 %slice-start.2 = ((s8[4718592]{0:T(1024)(128)(4,1)}), s8[4194304]{0:T(1024)(128)(4,1)S(1)}, s32[]{:S(2)}) async-start(s8[4718592]{0:T(1024)(128)(4,1)} %bitcast.230), calls=%async_computation.15 | async-start | bytes 8388608
  280.4 4.8 slice-start.3
  280.4 4.8 copy-start.60
  381.5 5.3 copy-start.29
  381.5 9.0 %collective-permute-start.2 = (f32[64,1152]{1,0:T(8,128)}, f32[64,1152]{1,0:T(8,128)}, u32[]{:S(2)}, u32[]{:S(2)}) collective-permute-start(f32[64,1152]{1,0:T(8,128)} %copy.184), channel_id=1, source_target_pairs={{0,1},{1,0},{2,3},{3,2},{4,5},{5,4},{6,7},{7,6},{8,9},{9,8},{10,11... | collective-permute-start | bytes 884744 | tf_op jit(solution)/shard_map/ppermute | solution.py:129
  386.8 7.1 %copy-start.48 = (s32[64,8]{0,1:T(8,128)S(1)}, s32[64,8]{0,1:T(8,128)}, u32[]{:S(2)}) copy-start(s32[64,8]{0,1:T(8,128)} %copy-done.47) | copy-start | bytes 6148
  386.8 7.1 %copy-start.51 = (f32[1024]{0:T(1024)S(1)}, f32[1024]{0:T(1024)}, u32[]{:S(2)}) copy-start(f32[1024]{0:T(1024)} %param.23) | copy-start | bytes 12292
  386.8 7.1 %copy-start.57 = (f32[64]{0:T(128)S(1)}, f32[64]{0:T(128)}, u32[]{:S(2)}) copy-start(f32[64]{0:T(128)} %copy-done.56) | copy-start | bytes 772
  390.0 13.4 %collective-permute-start.1 = (f32[64,1024]{0,1:T(8,128)}, f32[64,1024]{0,1:T(8,128)}, u32[]{:S(2)}, u32[]{:S(2)}) collective-permute-start(f32[64,1024]{0,1:T(8,128)} %constant_dynamic-slice_fusion.3), channel_id=1, source_target_pairs={{0,1},{1,0},{2,3},{3,2},{4,5},{5,4},{6,7},{7,6},{8,9},{9,8},{10,11... | collective-permute-start | bytes 786440 | tf_op jit(solution)/shard_map/ppermute | solution.py:129
  393.9 19.3 %copy-start.45 = (f32[1,8,128]{2,1,0:T(8,128)S(1)}, f32[1,8,128]{2,1,0:T(8,128)}, u32[]{:S(2)}) copy-start(f32[1,8,128]{2,1,0:T(8,128)} %copy-done.44) | copy-start | bytes 12292
  403.4 11.0 %copy-start.23 = (bf16[128,4,64,1]{0,2,3,1:T(8,128)(2,1)S(1)}, bf16[128,4,64,1]{0,2,3,1:T(8,128)(2,1)}, u32[]{:S(2)}) copy-start(bf16[128,4,64,1]{0,2,3,1:T(8,128)(2,1)} %copy-done.22) | copy-start | bytes 196612
  411.4 8.5 %copy-start.31 = (f32[128,64]{0,1:T(8,128)S(1)}, f32[128,64]{0,1:T(8,128)}, u32[]{:S(2)}) copy-start(f32[128,64]{0,1:T(8,128)} %copy-done.30) | copy-start | bytes 98308
  413.0 7.2 %copy-start.43 = (f32[128,64]{0,1:T(8,128)S(1)}, f32[128,64]{0,1:T(8,128)}, u32[]{:S(2)}) copy-start(f32[128,64]{0,1:T(8,128)} %get-tuple-element.141) | copy-start | bytes 98308
  413.1 7.1 %copy-start.46 = (f32[1,8,128]{2,1,0:T(8,128)S(1)}, f32[1,8,128]{2,1,0:T(8,128)}, u32[]{:S(2)}) copy-start(f32[1,8,128]{2,1,0:T(8,128)} %copy-done.44) | copy-start | bytes 12292
  414.4 6.7 %copy-start.7 = (bf16[128,2048]{1,0:T(8,128)(2,1)S(1)}, bf16[128,2048]{1,0:T(8,128)(2,1)}, u32[]{:S(2)}) copy-start(bf16[128,2048]{1,0:T(8,128)(2,1)} %copy-done.6) | copy-start | bytes 1572868
  414.6 27.9 %all-to-all-start.4 = ((bf16[1,2,1024,256]{3,1,0,2:T(2,128)(2,1)}), bf16[1,2,1024,256]{3,1,0,2:T(2,128)(2,1)}, u32[]{:S(2)}, u32[]{:S(2)}) async-start(bf16[1,2,1024,256]{3,1,0,2:T(2,128)(2,1)} %copy.201), calls=%async_computation.4 | async-start | bytes 2097152 | tf_op jit(solution)/shard_map/all_to_all | solution.py:380
  419.6 95.9 %reduce-scatter.9.cloned.1.call-start = ((), (), s32[]{:S(2)}) async-start(), calls=%async_computation.12 | async-start | bytes 3342336
  442.5 41.9 %all-to-all-start.5 = ((bf16[1,2,1024,256]{3,1,0,2:T(2,128)(2,1)}), bf16[1,2,1024,256]{3,1,0,2:T(2,128)(2,1)S(1)}, u32[]{:S(2)}, u32[]{:S(2)}) async-start(bf16[1,2,1024,256]{3,1,0,2:T(2,128)(2,1)} %copy.203), calls=%async_computation.5 | async-start | bytes 2097152 | tf_op jit(solution)/shard_map/all_to_all | solution.py:380
  453.0 4.1 copy-start.27
  453.0 4.1 copy-start.32
  453.0 4.1 copy-start.40
  453.0 4.1 copy-start.42
  457.9 29.1 %copy-start.21 = (bf16[64,1024]{0,1:T(8,128)(2,1)S(1)}, bf16[64,1024]{0,1:T(8,128)(2,1)}, u32[]{:S(2)}) copy-start(bf16[64,1024]{0,1:T(8,128)(2,1)} %get-tuple-element.120) | copy-start | bytes 393220
  457.9 30.0 %copy-start.49 = (f32[1024]{0:T(1024)S(1)}, f32[1024]{0:T(1024)}, u32[]{:S(2)}) copy-start(f32[1024]{0:T(1024)} %param.18) | copy-start | bytes 12292
  457.9 30.0 %copy-start.55 = (f32[64]{0:T(128)S(1)}, f32[64]{0:T(128)}, u32[]{:S(2)}) copy-start(f32[64]{0:T(128)} %copy-done.54) | copy-start | bytes 772
  458.1 29.8 %collective-permute-start.3 = (f32[64,1024]{0,1:T(8,128)S(1)}, f32[64,1024]{0,1:T(8,128)}, u32[]{:S(2)}, u32[]{:S(2)}) collective-permute-start(f32[64,1024]{0,1:T(8,128)S(1)} %constant_dynamic-slice_fusion), channel_id=1, source_target_pairs={{0,1},{1,0},{2,3},{3,2},{4,5},{5,4},{6,7},{7,6},{8,9},{9,8},{10,11... | collective-permute-start | bytes 786440 | tf_op jit(solution)/shard_map/ppermute | solution.py:129
  484.4 5.1 copy-start.5
  485.3 5.3 %copy-start.52 = (f32[1024]{0:T(1024)S(1)}, f32[1024]{0:T(1024)}, u32[]{:S(2)}) copy-start(f32[1024]{0:T(1024)} %get-tuple-element.86) | copy-start | bytes 12292
  (14 other events, 14.3 us)
Sparse Core Ops, SparseCore 0:
  10.9 48.1 all-gather.3
  61.2 71.2 all-gather.5
  134.7 75.1 all-gather.7
  259.2 117.6 reduce-scatter.6
  425.3 84.0 reduce-scatter.8
